TPU v7x, 512 devices: a whole 4x8x8 slice. The times are simulated.
512 devices in a mesh: pipe: 8 (over x, core), dp: 64 (over y, z).
Axes of the slice: x: 4, y: 8, z: 8, core: 2. Of those that a mesh axis runs over, the one named last changes fastest.
Arguments:
- acts: bfloat16 [8, 4, 256, 16384], P('pipe', None, None, 'dp'), may hold values from -100 to 100
- act_slot: int32 [8, 4], P('pipe'), may hold values from 0 to 3, each once within a row
- norm_gain: bfloat16 [8, 16384], P('pipe', 'dp'), may hold values from 0.5 to 1.5
- branch_grad: bfloat16 [8, 4, 256, 16384], P('pipe', None, None, 'dp'), may hold values from -6 to 6
- hidden_grad: bfloat16 [8, 4, 256, 53248], P('pipe', None, None, 'dp'), may hold values from -0.29882812 to 0.29882812
- sketch_seed: int32 [8, 53248], P('pipe', 'dp'), may hold values from 1 to 65520
- basis_old: bfloat16 [8, 16384, 256], P('pipe', 'dp'), may hold values from -0.046875 to 0.046875
- moment_old: bfloat16 [8, 256, 53248], P('pipe', None, 'dp'), may hold values from -12 to 12
Outputs:
- input_grad: bfloat16 [8, 4, 256, 16384], P('pipe', None, None, 'dp')
- moment_new: bfloat16 [8, 256, 53248], P('pipe', None, 'dp')
Inputs may be any that keep to these rules, and one draw needn't show every extreme that they name: act_slot[s] names each storage slot once.
All inputs are finite; a program needn't handle non-finite values.
Results may differ from a plain program's by a relative error of at most 0.0059.
Values sent between devices are 32-bit elements; how exact they have to be, the bound alone decides.
A program may use at most 64 MiB of HBM per device.

v0:
```python
import jax
import jax.numpy as jnp
from jax import lax
from jax.sharding import PartitionSpec as P

D = 16384
R = 256


def passed_along(value, axis, steps):
    count = lax.axis_size(axis)
    leading, last = (max(0, -steps), min(count, count - steps))
    return lax.ppermute(value, axis, [(source, source + steps) for source in range(leading, last)])


def sketch_table(seed_row):
    columns = jnp.arange(1, R + 1, dtype=jnp.int32)
    levels = seed_row[:, None] * columns[None, :] % 65521
    return ((levels.astype(jnp.float32) - 32760.0) * (1.7320508 / 32760.0)).astype(jnp.bfloat16)


def local(acts, act_slot, norm_gain, branch_grad, hidden_grad, sketch_seed, basis_old, moment_old):
    highest = lax.Precision.HIGHEST
    stored = acts[0][act_slot[0]].astype(jnp.float32)
    gains = norm_gain[0].astype(jnp.float32)
    upstream = gains * branch_grad[0].astype(jnp.float32)
    squares, crossed_sum = lax.psum(
        (
            jnp.sum(stored * stored, -1, keepdims=True),
            jnp.sum(stored * upstream, -1, keepdims=True),
        ),
        "dp",
    )
    inverse = 1.0 / jnp.sqrt(squares / D + 1e-05)
    crossed = crossed_sum / D
    term = inverse * upstream - stored * (inverse * inverse * inverse * crossed)
    section_count = lax.axis_size("pipe")
    current = term
    for section_step in range(section_count - 1):
        current = term + passed_along(current, "pipe", -1)
    input_grad = current.astype(jnp.bfloat16)[None]
    features = stored.shape[-1]
    normed = (stored * inverse * gains).astype(jnp.bfloat16).reshape(-1, features)
    normed_wide = normed.astype(jnp.float32)
    row_count = normed.shape[0]
    hidden = hidden_grad[0].reshape(row_count, -1)
    sketch_part = jnp.dot(hidden, sketch_table(sketch_seed[0]), preferred_element_type=jnp.float32)
    sketched = lax.psum(sketch_part, "dp")
    sketch_rows = lax.dot_general(
        normed_wide, sketched, (((0,), (0,)), ((), ())), precision=highest
    )
    basis_local = basis_old[0].astype(jnp.float32)
    gram_matrix = lax.psum(jnp.dot(sketch_rows.T, sketch_rows, precision=highest), "dp")
    factor = jnp.linalg.cholesky(gram_matrix)
    basis_new = lax.linalg.triangular_solve(
        factor, sketch_rows, left_side=False, lower=True, transpose_a=True
    )
    rotation, projected = lax.psum(
        (
            jnp.dot(basis_new.T, basis_local, precision=highest),
            jnp.dot(normed_wide, basis_new, precision=highest),
        ),
        "dp",
    )
    low_rank = lax.dot_general(
        projected, hidden.astype(jnp.float32), (((0,), (0,)), ((), ())), precision=highest
    )
    moment_new = (
        0.9 * jnp.dot(rotation, moment_old[0].astype(jnp.float32), precision=highest)
        + 0.1 * low_rank
    ).astype(jnp.bfloat16)
    return (input_grad, moment_new[None])


def solution(mesh):
    in_specs = (
        P("pipe", None, None, "dp"),
        P("pipe", None),
        P("pipe", "dp"),
        P("pipe", None, None, "dp"),
        P("pipe", None, None, "dp"),
        P("pipe", "dp"),
        P("pipe", "dp", None),
        P("pipe", None, "dp"),
    )
    out_specs = (P("pipe", None, None, "dp"), P("pipe", None, "dp"))
    return jax.shard_map(local, mesh=mesh, in_specs=in_specs, out_specs=out_specs, check_vma=False)
```

profile of v0, /device:TPU:6, one launch (start us, length us, event | category | flops | bytes accessed | tf_op | source)
XLA Modules:
  0.0 744.4 jit_solution(2249221503233910676)
XLA Ops:
  10.6 151.9 %all-reduce.1 = (f32[4,256,1]{1,0,2:T(4,128)S(1)}, f32[4,256,1]{1,0,2:T(4,128)S(1)}) all-reduce(f32[4,256,1]{1,0,2:T(4,128)S(1)} %bitcast.92, f32[4,256,1]{1,0,2:T(4,128)S(1)} %bitcast.91), channel_id=1, replica_groups=mesh['pipe'=8,'dp'=64] {'dp'}, use_global_device_ids=true, to_apply=%region_3.0 | all-reduce | flops 2048 | bytes 16384 | tf_op jit(solution)/shard_map/psum | solution.py:27
  163.0 1.9 collective-permute-start
  164.9 2.8 copy.12
  167.7 1.6 copy.17
  169.3 7.9 %collective-permute-done = f32[4,256,256]{2,1,0:T(8,128)} collective-permute-done((f32[4,256,256]{2,1,0:T(8,128)S(1)}, f32[4,256,256]{2,1,0:T(8,128)}, u32[]{:S(2)}, u32[]{:S(2)}) %collective-permute-start) | collective-permute-done | bytes 1048608 | tf_op jit(solution)/shard_map/ppermute | solution.py:13
  177.2 2.3 add.94
  179.5 3.9 collective-permute-start.1
  183.5 2.3 convolution_bitcast_fusion
  185.8 10.3 %collective-permute-done.1 = f32[4,256,256]{2,1,0:T(8,128)} collective-permute-done((f32[4,256,256]{2,1,0:T(8,128)}, f32[4,256,256]{2,1,0:T(8,128)}, u32[]{:S(2)}, u32[]{:S(2)}) %collective-permute-start.1) | collective-permute-done | bytes 1048608 | tf_op jit(solution)/shard_map/ppermute | solution.py:13
  196.1 2.3 add.95
  198.4 4.1 collective-permute-start.2
  202.7 137.5 %all-reduce.7.cloned.1.call-done = f32[1024,256]{0,1:T(8,128)} async-done(((f32[1024,256]{0,1:T(8,128)}), f32[1024,256]{0,1:T(8,128)}) %all-reduce.7.cloned.1.call-update) | async-done | bytes 1048592 | tf_op jit(solution)/shard_map/psum | solution.py:48
  340.2 2.0 fusion.48
  343.6 150.7 %all-reduce.9.cloned.1.call-done = f32[256,256]{0,1:T(8,128)} async-done(((f32[256,256]{0,1:T(8,128)}), f32[256,256]{0,1:T(8,128)}) %all-reduce.9.cloned.1.call-update) | async-done | bytes 262160 | tf_op jit(solution)/shard_map/psum | solution.py:53
  496.4 11.7 %cholesky.50 = f32[128,128]{1,0:T(8,128)S(1)} custom-call(f32[128,128]{1,0:T(8,128)S(1)} %cholesky.118), custom_call_target="Cholesky" | custom-call | tf_op jit(solution)/shard_map/jit(cholesky)/cholesky | solution.py:54
  508.1 2.3 add.96
  510.4 2.1 collective-permute-start.3
  512.6 9.8 %custom-call.14 = f32[1,128,128]{1,2,0:T(8,128)S(1)} custom-call(f32[1,128,128]{2,1,0:T(8,128)S(1)} %get-tuple-element.29), custom_call_target="InvertDiagBlocksLowerTriangular" | custom-call | tf_op jit(solution)/shard_map/jit(cholesky)/cholesky | solution.py:54
  522.9 11.7 %cholesky.105 = f32[128,128]{1,0:T(8,128)S(1)} custom-call(f32[128,128]{1,0:T(8,128)S(1)} %convolution_subtract_fusion.1), custom_call_target="Cholesky" | custom-call | tf_op jit(solution)/shard_map/jit(cholesky)/cholesky | solution.py:54
  536.6 2.3 add.97
  538.9 2.9 collective-permute-start.4
  541.8 3.8 while.1
  545.7 19.7 %custom-call.15 = f32[2,128,128]{1,2,0:T(8,128)S(1)} custom-call(f32[2,128,128]{2,1,0:T(8,128)S(1)} %get-tuple-element.9), custom_call_target="InvertDiagBlocksLowerTriangular" | custom-call | tf_op jit(solution)/shard_map/triangular_solve | solution.py:55
  566.4 2.4 add.98
  568.8 1.9 collective-permute-start.5
  571.7 1.6 fusion.26
  573.4 10.0 %collective-permute-done.5 = f32[4,256,256]{2,1,0:T(8,128)} collective-permute-done((f32[4,256,256]{2,1,0:T(8,128)}, f32[4,256,256]{2,1,0:T(8,128)}, u32[]{:S(2)}, u32[]{:S(2)}) %collective-permute-start.5) | collective-permute-done | bytes 1048608 | tf_op jit(solution)/shard_map/ppermute | solution.py:13
  583.3 2.4 add.99
  585.7 3.8 collective-permute-start.6
  589.5 142.1 %all-reduce.11.cloned.1.call-done = (f32[1024,256]{1,0:T(8,128)}, f32[256,256]{1,0:T(8,128)}) async-done(((f32[1024,256]{1,0:T(8,128)}, f32[256,256]{1,0:T(8,128)}), (f32[1024,256]{1,0:T(8,128)}, f32[256,256]{1,0:T(8,128)})) %all-reduce.11.cloned.1.call-update) | async-done | bytes 1310736 | tf_op jit(solution)/shard_map/psum | solution.py:58
  731.6 2.9 convolution_multiply_fusion
  735.8 2.1 fusion.16
  (62 shorter events, 16.0 us)
Async XLA Ops:
  7.2 1.5 copy-start
  7.2 155.4 %copy-start.3 = (bf16[1,4,256,256]{3,2,1,0:T(8,128)(2,1)S(1)}, bf16[1,4,256,256]{3,2,1,0:T(8,128)(2,1)}, u32[]{:S(2)}) copy-start(bf16[1,4,256,256]{3,2,1,0:T(8,128)(2,1)} %param.11) | copy-start | bytes 1572868
  7.2 333.0 %all-reduce.7.cloned.1.call-start = ((), (), s32[]{:S(2)}) async-start(), calls=%async_computation | async-start | bytes 2097152 | tf_op jit(solution)/shard_map/psum | solution.py:48
  163.0 14.2 %collective-permute-start = (f32[4,256,256]{2,1,0:T(8,128)S(1)}, f32[4,256,256]{2,1,0:T(8,128)}, u32[]{:S(2)}, u32[]{:S(2)}) collective-permute-start(f32[4,256,256]{2,1,0:T(8,128)S(1)} %fusion.5), channel_id=1, source_target_pairs={{64,0},{128,64},{192,128},{256,192},{320,256},{384,320},{448,384},... | collective-permute-start | bytes 3145736 | tf_op jit(solution)/shard_map/ppermute | solution.py:13
  167.7 1.6 copy-start.7
  169.3 14.2 %copy-start.1 = (bf16[104,8,4,256]{3,1,2,0:T(8,128)(2,1)S(1)}, bf16[104,8,4,256]{3,1,2,0:T(8,128)(2,1)}, u32[]{:S(2)}) copy-start(bf16[104,8,4,256]{3,1,2,0:T(8,128)(2,1)} %copy.17) | copy-start | bytes 5111812
  179.5 16.5 %collective-permute-start.1 = (f32[4,256,256]{2,1,0:T(8,128)}, f32[4,256,256]{2,1,0:T(8,128)}, u32[]{:S(2)}, u32[]{:S(2)}) collective-permute-start(f32[4,256,256]{2,1,0:T(8,128)} %add.94), channel_id=1, source_target_pairs={{64,0},{128,64},{192,128},{256,192},{320,256},{384,320},{448,384},... | collective-permute-start | bytes 3145736 | tf_op jit(solution)/shard_map/ppermute | solution.py:13
  185.7 308.5 %all-reduce.9.cloned.1.call-start = ((), (), s32[]{:S(2)}) async-start(), calls=%async_computation.1 | async-start | bytes 524288 | tf_op jit(solution)/shard_map/psum | solution.py:53
  198.4 309.7 %collective-permute-start.2 = (f32[4,256,256]{2,1,0:T(8,128)}, f32[4,256,256]{2,1,0:T(8,128)}, u32[]{:S(2)}, u32[]{:S(2)}) collective-permute-start(f32[4,256,256]{2,1,0:T(8,128)} %add.95), channel_id=1, source_target_pairs={{64,0},{128,64},{192,128},{256,192},{320,256},{384,320},{448,384},... | collective-permute-start | bytes 3145736 | tf_op jit(solution)/shard_map/ppermute | solution.py:13
  343.5 388.0 %all-reduce.11.cloned.1.call-start = ((), (), s32[]{:S(2)}) async-start(), calls=%async_computation.2 | async-start | bytes 2621440 | tf_op jit(solution)/shard_map/psum | solution.py:58
  510.4 26.1 %collective-permute-start.3 = (f32[4,256,256]{2,1,0:T(8,128)}, f32[4,256,256]{2,1,0:T(8,128)}, u32[]{:S(2)}, u32[]{:S(2)}) collective-permute-start(f32[4,256,256]{2,1,0:T(8,128)} %add.96), channel_id=1, source_target_pairs={{64,0},{128,64},{192,128},{256,192},{320,256},{384,320},{448,384},... | collective-permute-start | bytes 3145736 | tf_op jit(solution)/shard_map/ppermute | solution.py:13
  538.9 27.5 %collective-permute-start.4 = (f32[4,256,256]{2,1,0:T(8,128)}, f32[4,256,256]{2,1,0:T(8,128)}, u32[]{:S(2)}, u32[]{:S(2)}) collective-permute-start(f32[4,256,256]{2,1,0:T(8,128)} %add.97), channel_id=1, source_target_pairs={{64,0},{128,64},{192,128},{256,192},{320,256},{384,320},{448,384},... | collective-permute-start | bytes 3145736 | tf_op jit(solution)/shard_map/ppermute | solution.py:13
  566.1 4.6 copy-start.6
  568.8 14.5 %collective-permute-start.5 = (f32[4,256,256]{2,1,0:T(8,128)}, f32[4,256,256]{2,1,0:T(8,128)}, u32[]{:S(2)}, u32[]{:S(2)}) collective-permute-start(f32[4,256,256]{2,1,0:T(8,128)} %add.98), channel_id=1, source_target_pairs={{64,0},{128,64},{192,128},{256,192},{320,256},{384,320},{448,384},... | collective-permute-start | bytes 3145736 | tf_op jit(solution)/shard_map/ppermute | solution.py:13
  573.3 158.2 %copy-start.2 = (bf16[104,8,4,256]{3,1,2,0:T(8,128)(2,1)S(1)}, bf16[104,8,4,256]{3,1,2,0:T(8,128)(2,1)}, u32[]{:S(2)}) copy-start(bf16[104,8,4,256]{3,1,2,0:T(8,128)(2,1)} %copy.17) | copy-start | bytes 5111812
  585.7 150.1 %collective-permute-start.6 = (f32[4,256,256]{2,1,0:T(8,128)}, f32[4,256,256]{2,1,0:T(8,128)}, u32[]{:S(2)}, u32[]{:S(2)}) collective-permute-start(f32[4,256,256]{2,1,0:T(8,128)} %add.99), channel_id=1, source_target_pairs={{64,0},{128,64},{192,128},{256,192},{320,256},{384,320},{448,384},... | collective-permute-start | bytes 3145736 | tf_op jit(solution)/shard_map/ppermute | solution.py:13
  731.6 2.9 copy-start.4
  731.6 2.9 copy-start.5
Sparse Core Ops, SparseCore 0:
  185.9 154.3 all-reduce.6
  344.0 150.2 all-reduce.8
  573.5 158.0 all-reduce.10
where the time goes:
time: 745 us; the launch traced here: 744 us
  waiting for transfers between devices  458 us (61%)
  blocking collectives  152 us (20%)
  other arithmetic  74.3 us (10%)
  starting transfers between devices  20.7 us (3%)
  between operations  15.3 us (2%)
  matrix products  13.8 us (2%)
  local copies, waits for them, and re-layouts  9.97 us (1%)
    psum x1, blocking collectives, local(): lax.psum((jnp.sum(stored * stored, -1, keepdims=True), jnp.sum(stored * u...  152 us
    psum x1, waiting for transfers between devices, local(): lax.psum(jnp.dot(sketch_rows.T, sketch_rows, precision=highest), 'dp')  151 us
    psum x1, waiting for transfers between devices, local(): lax.psum((jnp.dot(basis_new.T, basis_local, precision=highest), jnp.dot(n...  142 us
    psum x1, waiting for transfers between devices, local(): sketched = lax.psum(sketch_part, 'dp')  137 us
    another operation x6, other arithmetic, local(): factor = jnp.linalg.cholesky(gram_matrix)  34 us
    ppermute x7, waiting for transfers between devices, passed_along(): lax.ppermute(value, axis, [(source, source + steps) for source in range(l...  28.1 us
    ppermute x7, starting transfers between devices, passed_along(): lax.ppermute(value, axis, [(source, source + steps) for source in range(l...  20.6 us
    another operation x3, other arithmetic, local(): lax.linalg.triangular_solve(factor, sketch_rows, left_side=False, lower=T...  19.7 us
  transfers between devices with their start and end apart: 10, of which 6 were waited for; matrix products, arithmetic and copies ran while one was open for 11% of the time, Pallas kernels for 0%

commit v1 on v0

v1 whole, which is shorter than its diff:
```python
import functools

import jax
import jax.numpy as jnp
from jax import lax
from jax.experimental import pallas as pl
from jax.experimental.pallas import tpu as pltpu
from jax.sharding import PartitionSpec as P

D = 16384
R = 256
MESH = pl.DeviceIdType.MESH
HIGHEST = lax.Precision.HIGHEST
PARTS = 2


class Place:
    def __init__(self, side):
        self.side = side
        self.pipe = lax.axis_index("pipe")
        dp = lax.axis_index("dp")
        self.y, self.z = dp // side, dp % side
        self.core = self.pipe % 2
        self.x = self.pipe // 2
        self.turn = 1 - 2 * self.core

    def wrap(self, value):
        return (value + 2 * self.side) % self.side

    def along(self, axis, steps):
        if axis == 0:
            return (self.pipe, self.wrap(self.y + steps) * self.side + self.z)
        return (self.pipe, self.y * self.side + self.wrap(self.z + steps))

    def at(self, axis):
        return self.y if axis == 0 else self.z


def greet(others):
    barrier = pltpu.get_barrier_semaphore()
    for other in others:
        pl.semaphore_signal(barrier, inc=1, device_id=other, device_id_type=MESH)
    pl.semaphore_wait(barrier, len(others))


def send(source, target, send_sem, recv_sem, device):
    copy = pltpu.make_async_remote_copy(
        src_ref=source, dst_ref=target, send_sem=send_sem, recv_sem=recv_sem,
        device_id=device, device_id_type=MESH,
    )
    copy.start()
    return copy


class Reduce:
    def __init__(self, place, x_ref, out_ref, ahead, behind, total, near, sems):
        self.p, self.x, self.out = place, x_ref, out_ref
        self.ahead, self.behind, self.total, self.near = ahead, behind, total, near
        (self.ring_s, self.ring_r, self.near_s, self.near_r,
         self.back_s, self.back_r, self.gather_s, self.gather_r) = sems
        side = place.side
        self.forward, self.backward = side // 2, side // 2 - 1
        self.chunk = x_ref.shape[0] // side
        self.piece = self.chunk // PARTS
        self.sub = self.chunk // side
        self.copies = []

    def cols(self, half):
        return pl.ds(128 * half, 128)

    def rows(self, index, part):
        return pl.ds(pl.multiple_of(index * self.chunk + part * self.piece, 8), self.piece)

    def ring_send(self, half, way, step, part):
        p, steps = self.p, (self.forward, self.backward)[way]
        if step >= steps:
            return
        sign = p.turn if way == 0 else -p.turn
        index = p.wrap(p.at(half) + sign * (steps - step))
        held = (self.ahead, self.behind)[way]
        here = pl.ds(part * self.piece, self.piece)
        own = self.x.at[self.rows(index, part), self.cols(half)]
        if step == 0:
            source = own
        else:
            source = held.at[half, step - 1, here]
            source[...] = source[...] + own[...]
        self.copies.append(send(
            source, held.at[half, step, here],
            self.ring_s.at[half, way, step, part], self.ring_r.at[half, way, step, part],
            p.along(half, sign)))

    def ring_wait(self, half, way, step, part):
        held = (self.ahead, self.behind)[way]
        here = held.at[half, step, pl.ds(part * self.piece, self.piece)]
        pltpu.make_async_copy(here, here, self.ring_r.at[half, way, step, part]).wait()

    def scatter_start(self):
        for part in range(PARTS):
            for half in range(2):
                for way in range(2):
                    self.ring_send(half, way, 0, part)

    def scatter_step(self, step):
        for part in range(PARTS):
            for half in range(2):
                for way in range(2):
                    if step < (self.forward, self.backward)[way]:
                        self.ring_wait(half, way, step, part)
                        self.ring_send(half, way, step + 1, part)

    def near_start(self):
        p = self.p
        for half in range(2):
            mine = pl.ds(pl.multiple_of(p.at(half) * self.chunk, 8), self.chunk)
            self.total[half] = (self.x[mine, self.cols(half)] + self.ahead[half, self.forward - 1]
                                + self.behind[half, self.backward - 1])
            for steps in range(1, p.side):
                there = p.wrap(p.at(1 - half) + steps)
                self.copies.append(send(
                    self.total.at[half, pl.ds(pl.multiple_of(there * self.sub, 8), self.sub)],
                    self.near.at[half, steps - 1],
                    self.near_s.at[half, steps - 1], self.near_r.at[half, steps - 1],
                    p.along(1 - half, steps)))

    def block(self, half):
        p = self.p
        start = p.at(half) * self.chunk + p.at(1 - half) * self.sub
        return pl.ds(pl.multiple_of(start, 8), self.sub)

    def near_end(self):
        p = self.p
        for half in range(2):
            mine = pl.ds(pl.multiple_of(p.at(1 - half) * self.sub, 8), self.sub)
            value = self.total[half, mine]
            for steps in range(1, p.side):
                slot = self.near.at[half, steps - 1]
                pltpu.make_async_copy(slot, slot, self.near_r.at[half, steps - 1]).wait()
                value = value + self.near[half, steps - 1]
            place = self.out.at[self.block(half), self.cols(half)]
            place[...] = value
            for steps in range(1, p.side):
                self.copies.append(send(
                    place, place, self.back_s.at[half, steps - 1], self.back_r.at[half, steps - 1],
                    p.along(1 - half, steps)))

    def back_end(self):
        p = self.p
        for half in range(2):
            for steps in range(1, p.side):
                start = p.at(half) * self.chunk + p.wrap(p.at(1 - half) - steps) * self.sub
                slot = self.out.at[pl.ds(pl.multiple_of(start, 8), self.sub), self.cols(half)]
                pltpu.make_async_copy(slot, slot, self.back_r.at[half, steps - 1]).wait()

    def gather_send(self, half, way, step, part):
        p = self.p
        if step >= (self.forward, self.backward)[way]:
            return
        sign = p.turn if way == 0 else -p.turn
        index = p.wrap(p.at(half) - sign * step)
        place = self.out.at[self.rows(index, part), self.cols(half)]
        self.copies.append(send(
            place, place, self.gather_s.at[half, way, step, part],
            self.gather_r.at[half, way, step, part], p.along(half, sign)))

    def gather_start(self):
        for part in range(PARTS):
            for half in range(2):
                for way in range(2):
                    self.gather_send(half, way, 0, part)

    def gather_step(self, step):
        p = self.p
        for part in range(PARTS):
            for half in range(2):
                for way in range(2):
                    if step < (self.forward, self.backward)[way]:
                        sign = p.turn if way == 0 else -p.turn
                        index = p.wrap(p.at(half) - sign * (step + 1))
                        place = self.out.at[self.rows(index, part), self.cols(half)]
                        pltpu.make_async_copy(
                            place, place, self.gather_r.at[half, way, step, part]).wait()
                        self.gather_send(half, way, step + 1, part)

    def finish(self):
        for copy in self.copies:
            copy.wait_send()


def reduce_scratch(rows, side):
    chunk = rows // side
    dma = pltpu.SemaphoreType.DMA
    return [
        pltpu.VMEM((2, side // 2, chunk, 128), jnp.float32),
        pltpu.VMEM((2, side // 2 - 1, chunk, 128), jnp.float32),
        pltpu.VMEM((2, chunk, 128), jnp.float32),
        pltpu.VMEM((2, side - 1, chunk // side, 128), jnp.float32),
        dma((2, 2, side // 2, PARTS)), dma((2, 2, side // 2, PARTS)),
        dma((2, side - 1)), dma((2, side - 1)),
        dma((2, side - 1)), dma((2, side - 1)),
        dma((2, 2, side // 2, PARTS)), dma((2, 2, side // 2, PARTS)),
    ]


def dp_peers(p):
    return [p.along(axis, steps) for axis in range(2) for steps in range(1, p.side)]


def first_kernel(side, x_ref, stat_ref, out_ref, stat_out, ahead, behind, total, near,
                 a, b, c, d, e, f, g, h, stat_slots, stat_mid, stat_s, stat_r):
    p = Place(side)
    greet(dp_peers(p))
    job = Reduce(p, x_ref, out_ref, ahead, behind, total, near, (a, b, c, d, e, f, g, h))
    copies = []

    def stat_send(source, axis):
        for steps in range(1, side):
            copies.append(send(
                source, stat_slots.at[axis, steps - 1], stat_s.at[axis, steps - 1],
                stat_r.at[axis, steps - 1], p.along(axis, steps)))

    def stat_sum(value, axis):
        for steps in range(1, side):
            slot = stat_slots.at[axis, steps - 1]
            pltpu.make_async_copy(slot, slot, stat_r.at[axis, steps - 1]).wait()
            value = value + stat_slots[axis, steps - 1]
        return value

    stat_send(stat_ref, 0)
    job.scatter_start()
    for step in range(job.forward):
        job.scatter_step(step)
        if step == 1:
            stat_mid[...] = stat_sum(stat_ref[...], 0)
            stat_send(stat_mid, 1)
    job.near_start()
    job.near_end()
    stat_out[...] = stat_sum(stat_mid[...], 1)
    job.back_end()
    job.gather_start()
    for step in range(job.forward):
        job.gather_step(step)
    job.finish()
    for copy in copies:
        copy.wait_send()


def first_reduce(x, stats, side):
    rows = x.shape[0]
    vmem = pl.BlockSpec(memory_space=pltpu.VMEM)
    dma = pltpu.SemaphoreType.DMA
    return pl.pallas_call(
        functools.partial(first_kernel, side),
        out_shape=(jax.ShapeDtypeStruct(x.shape, jnp.float32),
                   jax.ShapeDtypeStruct(stats.shape, jnp.float32)),
        in_specs=[vmem, vmem],
        out_specs=(vmem, vmem),
        scratch_shapes=reduce_scratch(rows, side) + [
            pltpu.VMEM((2, side - 1) + stats.shape, jnp.float32),
            pltpu.VMEM(stats.shape, jnp.float32),
            dma((2, side - 1)), dma((2, side - 1)),
        ],
        compiler_params=pltpu.CompilerParams(collective_id=1, has_side_effects=True),
        name="first_reduce",
    )(x, stats)


CHAIN = 4


def second_kernel(side, chips, x_ref, term_ref, out_ref, g_ref, ahead, behind, total, near,
                  a, b, c, d, e, f, g, h, other, above, pair_s, pair_r, down_s, down_r,
                  give_s, give_r, held):
    p = Place(side)
    dp = p.y * side + p.z
    partner = (p.x * 2 + 1 - p.core, dp)
    upper = (((p.x + 1) % chips) * 2 + p.core, dp)
    lower = (((p.x + chips - 1) % chips) * 2 + p.core, dp)
    greet(dp_peers(p) + [partner, upper, lower])
    job = Reduce(p, x_ref, out_ref, ahead, behind, total, near, (a, b, c, d, e, f, g, h))
    half_rows = term_ref.shape[0] // 2
    size = half_rows // CHAIN

    def rows(core, index):
        return pl.ds(pl.multiple_of(core * half_rows + index * size, 8), size)

    def pair_copy(index):
        here = pl.ds(pl.multiple_of(index * size, 8), size)
        return pltpu.make_async_remote_copy(
            src_ref=term_ref.at[rows(1 - p.core, index)], dst_ref=other.at[here],
            send_sem=pair_s.at[index], recv_sem=pair_r.at[index],
            device_id=partner, device_id_type=MESH)

    def down_copy(index):
        here = pl.ds(pl.multiple_of(index * size, 8), size)
        return pltpu.make_async_remote_copy(
            src_ref=held.at[here], dst_ref=above.at[here],
            send_sem=down_s.at[index], recv_sem=down_r.at[index],
            device_id=lower, device_id_type=MESH)

    def give_copy(index):
        place = g_ref.at[rows(p.core, index)]
        here = pl.ds(pl.multiple_of(half_rows + index * size, 8), size)
        return pltpu.make_async_remote_copy(
            src_ref=held.at[here], dst_ref=place,
            send_sem=give_s.at[index], recv_sem=give_r.at[index],
            device_id=partner, device_id_type=MESH)

    def chain_slot(slot):
        for shift in range(chips):
            index = slot - shift
            if 0 <= index < CHAIN:
                @pl.when(p.x == chips - 1 - shift)
                def _():
                    here = pl.ds(index * size, size)
                    pair_copy(index).wait_recv()
                    own = term_ref[rows(p.core, index)]
                    mate = other[here]
                    if shift > 0:
                        down_copy(index).wait_recv()
                        own_sum = own + above[here]
                        mate_sum = mate + above[here]
                    else:
                        own_sum, mate_sum = own, mate
                    both = own_sum + mate
                    lead = p.core == 0
                    held[here] = both
                    held[pl.ds(half_rows + index * size, size)] = jnp.where(lead, mate_sum, both)
                    g_ref[rows(p.core, index)] = jnp.where(lead, both, own_sum)
                    if shift < chips - 1:
                        down_copy(index).start()
                    give_copy(index).start()

    for index in range(CHAIN):
        pair_copy(index).start()
    job.scatter_start()
    for step in range(job.forward):
        job.scatter_step(step)
        chain_slot(step)
    job.near_start()
    chain_slot(4)
    job.near_end()
    chain_slot(5)
    job.back_end()
    job.gather_start()
    chain_slot(6)
    for step in range(job.forward):
        job.gather_step(step)
    for index in range(CHAIN):
        pair_copy(index).wait_send()
        give_copy(index).wait_send()
        place = g_ref.at[rows(1 - p.core, index)]
        pltpu.make_async_copy(place, place, give_r.at[index]).wait()

    @pl.when(p.x > 0)
    def _():
        for index in range(CHAIN):
            down_copy(index).wait_send()

    job.finish()


def second_reduce(x, term, side, chips):
    rows = x.shape[0]
    vmem = pl.BlockSpec(memory_space=pltpu.VMEM)
    dma = pltpu.SemaphoreType.DMA
    half = (term.shape[0] // 2, term.shape[1])
    return pl.pallas_call(
        functools.partial(second_kernel, side, chips),
        out_shape=(jax.ShapeDtypeStruct(x.shape, jnp.float32),
                   jax.ShapeDtypeStruct(term.shape, jnp.float32)),
        in_specs=[vmem, vmem],
        out_specs=(vmem, vmem),
        scratch_shapes=reduce_scratch(rows, side) + [
            pltpu.VMEM(half, jnp.float32), pltpu.VMEM(half, jnp.float32),
            dma((CHAIN,)), dma((CHAIN,)), dma((CHAIN,)), dma((CHAIN,)),
            dma((CHAIN,)), dma((CHAIN,)),
            pltpu.VMEM(term.shape, jnp.float32),
        ],
        compiler_params=pltpu.CompilerParams(collective_id=2, has_side_effects=True),
        name="second_reduce",
    )(x, term)


PANEL = 32


def factor_kernel(gram_ref, inverse_ref, upper, work):
    width = PANEL
    row = lax.broadcasted_iota(jnp.int32, (width, 128), 0)
    lane = lax.broadcasted_iota(jnp.int32, (width, 128), 1)
    for panel in range(R // width):
        start = panel * width
        here = pl.ds(start, width)
        block = gram_ref[here, :]
        wide = lax.broadcasted_iota(jnp.int32, (width, R), 1)
        deep = lax.broadcasted_iota(jnp.int32, (width, R), 0)
        target = jnp.where(wide == deep + start, 1.0, 0.0).astype(jnp.float32)
        if panel > 0:
            left = upper[pl.ds(0, start), :][:, start:start + width]
            block = block - lax.dot_general(left, upper[pl.ds(0, start), :], (((0,), (0,)), ((), ())),
                                            precision=HIGHEST, preferred_element_type=jnp.float32)
            target = target - lax.dot_general(left, inverse_ref[pl.ds(0, start), :],
                                              (((0,), (0,)), ((), ())), precision=HIGHEST,
                                              preferred_element_type=jnp.float32)
        tile = block[:, start:start + width]
        work[...] = jnp.where(lane == row + width, 1.0, 0.0).astype(jnp.float32)
        work[:, 0:width] = tile
        value = work[...]
        for k in range(width):
            column = jnp.broadcast_to(value[:, k:k + 1], (width, 128))
            scale = lax.rsqrt(column[k:k + 1, :])
            pivot_row = value[k:k + 1, :] * scale
            weights = jnp.where(row > k, column, 0.0) * scale
            value = jnp.where(row == k, pivot_row, value - weights * pivot_row)
        corner = value[:, width:2 * width]
        upper[here, :] = jnp.dot(corner, block, precision=HIGHEST, preferred_element_type=jnp.float32)
        inverse_ref[here, :] = jnp.dot(corner, target, precision=HIGHEST,
                                       preferred_element_type=jnp.float32)


def factor_inverse(gram):
    vmem = pl.BlockSpec(memory_space=pltpu.VMEM)
    return pl.pallas_call(
        factor_kernel,
        out_shape=jax.ShapeDtypeStruct((R, R), jnp.float32),
        in_specs=[vmem],
        out_specs=vmem,
        scratch_shapes=[pltpu.VMEM((R, R), jnp.float32), pltpu.VMEM((PANEL, 128), jnp.float32)],
        name="factor_inverse",
    )(gram)


def sketch_table(seed_row):
    columns = jnp.arange(1, R + 1, dtype=jnp.int32)
    levels = seed_row[:, None] * columns[None, :] % 65521
    return ((levels.astype(jnp.float32) - 32760.0) * (1.7320508 / 32760.0)).astype(jnp.bfloat16)


def local(side, acts, act_slot, norm_gain, branch_grad, hidden_grad, sketch_seed, basis_old, moment_old):
    stored = acts[0][act_slot[0]].astype(jnp.float32)
    gains = norm_gain[0].astype(jnp.float32)
    upstream = gains * branch_grad[0].astype(jnp.float32)
    features = stored.shape[-1]
    tokens = stored.shape[0] * stored.shape[1]
    squares_part = jnp.sum(stored * stored, -1).reshape(-1, 128)
    crossed_part = jnp.sum(stored * upstream, -1).reshape(-1, 128)
    hidden = hidden_grad[0].reshape(tokens, -1)
    sketch_part = jnp.dot(hidden, sketch_table(sketch_seed[0]), preferred_element_type=jnp.float32)
    sketched, stats = first_reduce(
        sketch_part, jnp.concatenate([squares_part, crossed_part], 0), side)
    shape = stored.shape[:-1] + (1,)
    squares = stats[:tokens // 128].reshape(shape)
    inverse = 1.0 / jnp.sqrt(squares / D + 1e-05)
    crossed = stats[tokens // 128:].reshape(shape) / D
    term = inverse * upstream - stored * (inverse * inverse * inverse * crossed)
    normed = (stored * inverse * gains).astype(jnp.bfloat16).reshape(tokens, features)
    normed_wide = normed.astype(jnp.float32)
    sketch_rows = lax.dot_general(
        normed_wide, sketched, (((0,), (0,)), ((), ())), precision=HIGHEST)
    stacked = jnp.concatenate(
        [normed_wide, basis_old[0].astype(jnp.float32).T, sketch_rows.T], 0)
    parts = jnp.dot(stacked, sketch_rows, precision=HIGHEST)
    chips = lax.axis_size("pipe") // 2
    sums, grad = second_reduce(parts, term.reshape(tokens, features), side, chips)
    input_grad = grad.astype(jnp.bfloat16).reshape(branch_grad.shape)
    pushed, cross, gram = sums[:tokens], sums[tokens:tokens + R], sums[tokens + R:]
    factor_inv = factor_inverse(gram)
    mixed = 0.9 * lax.dot_general(
        cross, moment_old[0].astype(jnp.float32), (((0,), (0,)), ((), ())), precision=HIGHEST
    ) + 0.1 * lax.dot_general(
        pushed, hidden.astype(jnp.float32), (((0,), (0,)), ((), ())), precision=HIGHEST)
    moment_new = jnp.dot(factor_inv, mixed, precision=HIGHEST).astype(jnp.bfloat16)
    return (input_grad, moment_new[None])


def solution(mesh):
    in_specs = (
        P("pipe", None, None, "dp"),
        P("pipe", None),
        P("pipe", "dp"),
        P("pipe", None, None, "dp"),
        P("pipe", None, None, "dp"),
        P("pipe", "dp"),
        P("pipe", "dp", None),
        P("pipe", None, "dp"),
    )
    out_specs = (P("pipe", None, None, "dp"), P("pipe", None, "dp"))
    side = int(round(mesh.shape["dp"] ** 0.5))
    return jax.shard_map(functools.partial(local, side), mesh=mesh, in_specs=in_specs,
                         out_specs=out_specs, check_vma=False)
```

time: 745 us -> 172 us (0.23)
  the two profiles are of different devices: /device:TPU:6 before, /device:TPU:8 now
where the time goes in v1:
time: 172 us
  Pallas kernels  141 us (82%)
  matrix products  16 us (9%)
  other arithmetic  7.81 us (5%)
  local copies, waits for them, and re-layouts  6.53 us (4%)
    pallas_call x1, Pallas kernels, first_reduce(): pl.pallas_call(functools.partial(first_kernel, side), out_shape=(jax.Shap...  57.2 us
    pallas_call x1, Pallas kernels, second_reduce(): pl.pallas_call(functools.partial(second_kernel, side, chips), out_shape=(...  56 us
    pallas_call x1, Pallas kernels, factor_inverse(): pl.pallas_call(factor_kernel, out_shape=jax.ShapeDtypeStruct((R, R), jnp....  27.5 us
    dot_general x1, matrix products, local(): lax.dot_general(pushed, hidden.astype(jnp.float32), (((0,), (0,)), ((), (...  4.74 us
    unnamed x19, local copies, waits for them, and re-layouts  4.26 us

profile of v1, /device:TPU:8, one launch (start us, length us, event | category | flops | bytes accessed | tf_op | source)
XLA Modules:
  0.0 171.8 jit_solution(1687413521529216316)
XLA Ops:
  0.6 0.0 copy-start
  0.6 0.0 copy-start.1
  0.7 1.0 copy-done
  1.7 0.7 fusion.33
  2.3 0.7 convert_element_type.74
  3.0 0.5 iota_add_fusion
  3.6 1.3 reduce
  4.9 1.0 copy.14
  5.9 0.6 gather_fusion
  6.5 0.0 copy-done.1
  6.5 0.4 fusion.12
  6.9 0.6 pad_maximum_fusion.stat_ref
  7.5 1.3 copy.12
  8.8 0.0 copy-start.6
  8.8 0.4 copy.16
  9.2 0.3 copy-done.6
  9.5 2.4 %convolution_bitcast_fusion.x_ref = f32[1024,256]{1,0:T(8,128)} fusion(bf16[1024,832]{0,1:T(8,128)(2,1)S(1)} %bitcast.61, s32[256]{0:T(256)S(1)} %copy-done.7, s32[832]{0:T(1024)S(1)} %copy-done.6), kind=kOutput, calls=%fused_computation.7 | convolution fusion | flops 438550528 | bytes 2756864 | tf_op jit(solution)/shard_map/dot_general | solution.py:449
  11.9 57.2 %first_reduce.1 = (f32[1024,256]{1,0:T(8,128)}, f32[16,128]{1,0:T(8,128)}) custom-call(f32[1024,256]{1,0:T(8,128)} %convolution_bitcast_fusion.x_ref, f32[16,128]{1,0:T(8,128)} %pad_maximum_fusion.stat_ref), custom_call_target="tpu_custom_call" | custom-call | tf_op jit(solution)/shard_map/first_reduce/pallas_call | solution.py:252
  69.1 0.7 fusion.32
  69.8 0.7 rsqrt_bitcast_fusion
  70.5 1.4 fusion.39
  71.9 1.0 fusion.41
  72.9 2.6 %fusion.x_ref = f32[1536,256]{1,0:T(8,128)} fusion(f32[256,256]{0,1:T(8,128)S(1)} %fusion.41, f32[256,256]{1,0:T(8,128)S(1)} %bitcast.64, f32[256,256]{1,0:T(8,128)S(1)} %convert_bitcast_fusion, f32[1024,256]{1,0:T(8,128)S(1)} %get-tuple-element.12), kind=kOutput, calls=%fused_computation.1 | convolution fusion | flops 1208745984 | bytes 3407872 | tf_op jit(solution)/shard_map/dot_general | solution.py:463
  75.5 56.0 %second_reduce.1 = (f32[1536,256]{1,0:T(8,128)}, f32[1024,256]{1,0:T(8,128)}) custom-call(f32[1536,256]{1,0:T(8,128)} %fusion.x_ref, f32[1024,256]{1,0:T(8,128)} %get-tuple-element.14.term_ref), custom_call_target="tpu_custom_call" | custom-call | tf_op jit(solution)/shard_map/second_reduce/pallas_call | solution.py:368
  131.6 4.7 %convolution_multiply_fusion.1 = f32[256,832]{1,0:T(8,128)S(1)} fusion(bf16[1024,832]{0,1:T(8,128)(2,1)S(1)} %bitcast.62, f32[1536,256]{1,0:T(8,128)} %get-tuple-element.9), kind=kOutput, calls=%fused_computation.10 | convolution fusion | flops 2617458688 | bytes 3604480 | tf_op jit(solution)/shard_map/dot_general | solution.py:471
  136.3 0.0 copy-start.5
  136.4 0.8 convert_element_type.71
  137.2 0.2 copy-done.5
  137.4 2.0 %fusion.6 = f32[256,832]{1,0:T(8,128)S(1)} fusion(f32[256,832]{1,0:T(8,128)S(1)} %convolution_multiply_fusion.1, bf16[1,256,832]{1,2,0:T(8,128)(2,1)S(1)} %copy-done.5, f32[1536,256]{1,0:T(8,128)} %get-tuple-element.9), kind=kOutput, calls=%fused_computation.9 | convolution fusion | flops 654737408 | bytes 2392064 | tf_op jit(solution)/shard_map/dot_general | solution.py:469
  139.4 1.7 slice.17.gram_ref
  141.1 27.5 %factor_inverse.1 = f32[256,256]{1,0:T(8,128)} custom-call(f32[256,256]{1,0:T(8,128)} %slice.17.gram_ref), custom_call_target="tpu_custom_call" | custom-call | tf_op jit(solution)/shard_map/factor_inverse/pallas_call | solution.py:424
  168.5 3.3 %fusion.7 = bf16[1,256,832]{1,2,0:T(8,128)(2,1)} fusion(f32[256,256]{1,0:T(8,128)} %factor_inverse.1, f32[256,832]{1,0:T(8,128)S(1)} %fusion.6), kind=kOutput, calls=%fused_computation.13 | convolution fusion | flops 654524416 | bytes 1540096 | tf_op jit(solution)/shard_map/dot_general | solution.py:473
  (12 shorter events, 0.1 us)
Async XLA Ops:
  0.6 1.0 copy-start
  0.6 5.8 %copy-start.1 = (bf16[1,4,256,256]{3,2,1,0:T(8,128)(2,1)S(1)}, bf16[1,4,256,256]{3,2,1,0:T(8,128)(2,1)}, u32[]{:S(2)}) copy-start(bf16[1,4,256,256]{3,2,1,0:T(8,128)(2,1)} %param.11) | copy-start | bytes 1572868
  0.7 6.8 %copy-start.2 = (bf16[1,4,256,832]{2,3,1,0:T(8,128)(2,1)S(1)}, bf16[1,4,256,832]{2,3,1,0:T(8,128)(2,1)}, u32[]{:S(2)}) copy-start(bf16[1,4,256,832]{2,3,1,0:T(8,128)(2,1)} %param.12) | copy-start | bytes 5111812
  8.8 0.7 copy-start.6
  8.8 0.7 copy-start.7
  70.5 1.4 copy-start.3
  131.6 4.8 %copy-start.4 = (f32[1024,256]{1,0:T(8,128)S(1)}, f32[1024,256]{1,0:T(8,128)}, u32[]{:S(2)}) copy-start(f32[1024,256]{1,0:T(8,128)} %get-tuple-element.8) | copy-start | bytes 3145732
  136.3 1.1 copy-start.5

commit v2 on v0

v2 whole, which is shorter than its diff:
```python
import functools

import jax
import jax.numpy as jnp
from jax import lax
from jax.experimental import pallas as pl
from jax.experimental.pallas import tpu as pltpu
from jax.sharding import PartitionSpec as P

D = 16384
R = 256
MESH = pl.DeviceIdType.MESH
HIGHEST = lax.Precision.HIGHEST
F32 = jnp.float32
BF16 = jnp.bfloat16
SIDE = 8
CHAIN = 4
PANEL = 32
FIRST = ((0,), (0,))
LAST = ((1,), (1,))
PLAIN = ((1,), (0,))


def dot(a, b, contract=PLAIN, precision=None):
    return lax.dot_general(a, b, (contract, ((), ())), precision=precision,
                           preferred_element_type=F32)


def split(value, count):
    parts = []
    for _ in range(count):
        part = value.astype(BF16)
        parts.append(part)
        value = value - part.astype(F32)
    return parts


class Place:
    def __init__(self):
        self.pipe = lax.axis_index("pipe")
        self.dp = lax.axis_index("dp")
        self.y, self.z = self.dp // SIDE, self.dp % SIDE
        self.core = self.pipe % 2
        self.x = self.pipe // 2
        self.turn = 1 - 2 * self.core

    def wrap(self, value):
        return (value + 2 * SIDE) % SIDE

    def along(self, axis, steps):
        if axis == 0:
            return (self.pipe, self.wrap(self.y + steps) * SIDE + self.z)
        return (self.pipe, self.y * SIDE + self.wrap(self.z + steps))

    def at(self, axis):
        return self.y if axis == 0 else self.z


def send(source, target, send_sem, recv_sem, device):
    pltpu.make_async_remote_copy(
        src_ref=source, dst_ref=target, send_sem=send_sem, recv_sem=recv_sem,
        device_id=device, device_id_type=MESH,
    ).start()


def await_bytes(like, sem):
    pltpu.make_async_copy(like, like, sem).wait()


class Reduce:
    def __init__(self, place, x, out, scratch):
        self.p, self.x, self.out = place, x, out
        self.tree, self.total, self.near, self.recv, self.sent = scratch
        self.chunk = x.shape[0] // SIDE
        self.sub = self.chunk // SIDE

    @staticmethod
    def scratch(rows):
        chunk = rows // SIDE
        return [
            pltpu.VMEM((2, 7, chunk, 128), F32),
            pltpu.VMEM((2, chunk, 128), F32),
            pltpu.VMEM((2, SIDE - 1, chunk // SIDE, 128), F32),
            pltpu.SemaphoreType.DMA((2, 8)),
            pltpu.SemaphoreType.DMA((2, 4)),
        ]

    def part(self, ref, half, index):
        rows = pl.ds(pl.multiple_of(index * self.chunk, 8), self.chunk)
        return ref.at[rows, pl.ds(128 * half, 128)]

    def owned(self, half, steps):
        p = self.p
        return p.wrap(p.at(half) + p.turn * steps)

    def tree_send(self, half, source, slot, sem, steps):
        p = self.p
        send(source, self.tree.at[half, slot], self.sent.at[half, 0], self.recv.at[half, sem],
             p.along(half, p.turn * steps))

    def scatter_start(self):
        for owner, slot, sem, steps in ((4, 0, 0, 2), (3, 1, 0, 1), (-3, 2, 1, -1),
                                        (1, 3, 2, 1), (-1, 4, 2, -1)):
            for half in range(2):
                self.tree_send(half, self.part(self.x, half, self.owned(half, owner)),
                               slot, sem, steps)

    def scatter_mid(self):
        for half in range(2):
            await_bytes(self.tree.at[half, 0:2], self.recv.at[half, 0])
            self.tree[half, 0] = (self.tree[half, 0] + self.tree[half, 1]
                                  + self.part(self.x, half, self.owned(half, 2))[...])
            self.tree_send(half, self.tree.at[half, 0], 5, 2, 2)
        for half in range(2):
            await_bytes(self.tree.at[half, 2], self.recv.at[half, 1])
            self.tree[half, 2] = (self.tree[half, 2]
                                  + self.part(self.x, half, self.owned(half, -2))[...])
            self.tree_send(half, self.tree.at[half, 2], 6, 2, -2)

    def scatter_end(self):
        p = self.p
        for half in range(2):
            await_bytes(self.tree.at[half, 3:7], self.recv.at[half, 2])
            value = self.part(self.x, half, p.at(half))[...]
            for slot in range(3, 7):
                value = value + self.tree[half, slot]
            self.total[half] = value
            for steps in (4, 3, 5, 2, 6, 1, 7):
                there = p.wrap(p.at(1 - half) + steps)
                send(self.total.at[half, pl.ds(pl.multiple_of(there * self.sub, 8), self.sub)],
                     self.near.at[half, steps - 1], self.sent.at[half, 1],
                     self.recv.at[half, 3], p.along(1 - half, steps))

    def near_end(self):
        p = self.p
        for half in range(2):
            await_bytes(self.near.at[half], self.recv.at[half, 3])
            value = self.total[half, pl.ds(pl.multiple_of(p.at(1 - half) * self.sub, 8), self.sub)]
            for slot in range(SIDE - 1):
                value = value + self.near[half, slot]
            start = p.at(half) * self.chunk + p.at(1 - half) * self.sub
            place = self.out.at[pl.ds(pl.multiple_of(start, 8), self.sub), pl.ds(128 * half, 128)]
            place[...] = value
            for steps in (4, 3, 5, 2, 6, 1, 7):
                send(place, place, self.sent.at[half, 2], self.recv.at[half, 4],
                     p.along(1 - half, steps))

    def gather_send(self, half, index, sem, steps):
        p = self.p
        place = self.part(self.out, half, index)
        send(place, place, self.sent.at[half, 3], self.recv.at[half, sem],
             p.along(half, p.turn * steps))

    def gather_start(self):
        for half in range(2):
            await_bytes(self.near.at[half], self.recv.at[half, 4])
            for sem, steps in ((5, 2), (6, -2), (7, 1), (7, -1)):
                self.gather_send(half, self.p.at(half), sem, steps)

    def gather_mid(self):
        for half in range(2):
            await_bytes(self.tree.at[half, 0], self.recv.at[half, 5])
            self.gather_send(half, self.owned(half, -2), 7, 2)
            self.gather_send(half, self.owned(half, -2), 7, 1)
        for half in range(2):
            await_bytes(self.tree.at[half, 0], self.recv.at[half, 6])
            self.gather_send(half, self.owned(half, 2), 7, -1)

    def gather_end(self):
        for half in range(2):
            await_bytes(self.tree.at[half, 0:5], self.recv.at[half, 7])

    def finish(self):
        for half in range(2):
            await_bytes(self.tree.at[half], self.sent.at[half, 0])
            await_bytes(self.near.at[half], self.sent.at[half, 1])
            await_bytes(self.near.at[half], self.sent.at[half, 2])
            await_bytes(self.tree.at[half], self.sent.at[half, 3])


class Small:
    def __init__(self, place, x, out, scratch):
        self.p, self.x, self.out = place, x, out
        self.slots, self.mid, self.recv, self.sent = scratch
        self.chunk = x.shape[0] // SIDE

    @staticmethod
    def scratch(rows):
        chunk = rows // SIDE
        return [
            pltpu.VMEM((2, 2, SIDE - 1, chunk, 128), F32),
            pltpu.VMEM((2, chunk, 128), F32),
            pltpu.SemaphoreType.DMA((2, 3)),
            pltpu.SemaphoreType.DMA((2, 3)),
        ]

    def part(self, ref, half, index):
        rows = pl.ds(pl.multiple_of(index * self.chunk, 8), self.chunk)
        return ref.at[rows, pl.ds(128 * half, 128)]

    def start(self):
        p = self.p
        for steps in (4, 3, 5, 2, 6, 1, 7):
            for half in range(2):
                send(self.part(self.x, half, p.wrap(p.at(half) + steps)),
                     self.slots.at[0, half, steps - 1], self.sent.at[half, 0],
                     self.recv.at[half, 0], p.along(half, steps))

    def total(self, stage, half, value):
        await_bytes(self.slots.at[stage, half], self.recv.at[half, stage])
        for slot in range(SIDE - 1):
            value = value + self.slots[stage, half, slot]
        return value

    def middle(self):
        p = self.p
        for half in range(2):
            self.mid[half] = self.total(0, half, self.part(self.x, half, p.at(half))[...])
            for steps in (4, 3, 5, 2, 6, 1, 7):
                send(self.mid.at[half], self.slots.at[1, half, steps - 1], self.sent.at[half, 1],
                     self.recv.at[half, 1], p.along(1 - half, steps))

    def spread(self):
        p = self.p
        for half in range(2):
            place = self.part(self.out, half, p.at(half))
            place[...] = self.total(1, half, self.mid[half])
            for steps in (4, 3, 5, 2, 6, 1, 7):
                send(place, place, self.sent.at[half, 2], self.recv.at[half, 2],
                     p.along(half, steps))

    def end(self):
        for half in range(2):
            await_bytes(self.slots.at[0, half], self.recv.at[half, 2])

    def finish(self):
        for half in range(2):
            for stage in range(3):
                await_bytes(self.slots.at[0, half], self.sent.at[half, stage])


class Stats:
    def __init__(self, place, tile, slots, mid, recv, sent):
        self.p, self.tile, self.slots, self.mid = place, tile, slots, mid
        self.recv, self.sent = recv, sent

    def push(self, source, axis):
        for steps in (4, 3, 5, 2, 6, 1, 7):
            send(source, self.slots.at[axis, steps - 1], self.sent.at[axis], self.recv.at[axis],
                 self.p.along(axis, steps))

    def total(self, source, axis):
        await_bytes(self.slots.at[axis], self.recv.at[axis])
        value = source[...]
        for slot in range(SIDE - 1):
            value = value + self.slots[axis, slot]
        return value

    def start(self):
        self.push(self.tile, 0)

    def middle(self):
        self.mid[...] = self.total(self.tile, 0)
        self.push(self.mid, 1)

    def end(self):
        return self.total(self.mid, 1)

    def finish(self):
        for axis in range(2):
            await_bytes(self.slots.at[axis], self.sent.at[axis])


class Chain:
    def __init__(self, place, chips, term, grad, other, above, held, sems):
        self.p, self.chips = place, chips
        self.term, self.grad, self.other, self.above, self.held = term, grad, other, above, held
        self.pair_s, self.pair_r, self.down_s, self.down_r, self.give_s, self.give_r = sems
        self.half_rows = term.shape[0] // 2
        self.size = self.half_rows // CHAIN
        self.partner, self.upper, self.lower = chain_peers(place, chips)

    def rows(self, core, index):
        return pl.ds(pl.multiple_of(core * self.half_rows + index * self.size, 8), self.size)

    def remote(self, source, target, send_sem, recv_sem, device):
        return pltpu.make_async_remote_copy(
            src_ref=source, dst_ref=target, send_sem=send_sem, recv_sem=recv_sem,
            device_id=device, device_id_type=MESH)

    def pair(self, index):
        here = pl.ds(index * self.size, self.size)
        return self.remote(self.term.at[self.rows(1 - self.p.core, index)], self.other.at[here],
                           self.pair_s.at[index], self.pair_r.at[index], self.partner)

    def down(self, index):
        here = pl.ds(index * self.size, self.size)
        return self.remote(self.held.at[here], self.above.at[here],
                           self.down_s.at[index], self.down_r.at[index], self.lower)

    def give(self, index):
        here = pl.ds(self.half_rows + index * self.size, self.size)
        return self.remote(self.held.at[here], self.grad.at[self.rows(self.p.core, index)],
                           self.give_s.at[index], self.give_r.at[index], self.partner)

    def start(self):
        for index in range(CHAIN):
            self.pair(index).start()

    def slot(self, slot):
        for shift in range(self.chips):
            index = slot - shift
            if 0 <= index < CHAIN:
                @pl.when(self.p.x == self.chips - 1 - shift)
                def _():
                    here = pl.ds(index * self.size, self.size)
                    self.pair(index).wait_recv()
                    own_sum = self.term[self.rows(self.p.core, index)]
                    mate = self.other[here]
                    mate_sum = mate
                    if shift > 0:
                        self.down(index).wait_recv()
                        own_sum = own_sum + self.above[here]
                        mate_sum = mate + self.above[here]
                    both = own_sum + mate
                    lead = self.p.core == 0
                    self.held[here] = both
                    self.held[pl.ds(self.half_rows + index * self.size, self.size)] = jnp.where(
                        lead, mate_sum, both)
                    self.grad[self.rows(self.p.core, index)] = jnp.where(lead, both, own_sum)
                    if shift < self.chips - 1:
                        self.down(index).start()
                    self.give(index).start()

    def end(self):
        for index in range(CHAIN):
            place = self.grad.at[self.rows(1 - self.p.core, index)]
            await_bytes(place, self.give_r.at[index])

    def finish(self):
        for index in range(CHAIN):
            self.pair(index).wait_send()
            self.give(index).wait_send()

        @pl.when(self.p.x > 0)
        def _():
            for index in range(CHAIN):
                self.down(index).wait_send()


def chain_peers(p, chips):
    return ((p.x * 2 + 1 - p.core, p.dp),
            (((p.x + 1) % chips) * 2 + p.core, p.dp),
            (((p.x + chips - 1) % chips) * 2 + p.core, p.dp))


def factor_panel(panel, gram, inverse, upper):
    width = PANEL
    start = panel * width
    here = pl.ds(start, width)
    row = lax.broadcasted_iota(jnp.int32, (width, 128), 0)
    lane = lax.broadcasted_iota(jnp.int32, (width, 128), 1)
    block = gram[here, :]
    wide = lax.broadcasted_iota(jnp.int32, (width, R), 1)
    deep = lax.broadcasted_iota(jnp.int32, (width, R), 0)
    target = jnp.where(wide == deep + start, 1.0, 0.0).astype(F32)
    if panel > 0:
        before = upper[0:start, :]
        left = before[:, start:start + width]
        block = block - dot(left, before, FIRST, HIGHEST)
        target = target - dot(left, inverse[0:start, :], FIRST, HIGHEST)
    tile = block[:, 128 * (start // 128):128 * (start // 128) + 128]
    shift = start % 128
    if shift:
        tile = pltpu.roll(tile, 128 - shift, 1)
    value = jnp.where(lane < width, tile, jnp.where(lane == row + width, 1.0, 0.0).astype(F32))
    for k in range(width):
        column = jnp.broadcast_to(value[:, k:k + 1], (width, 128))
        scale = lax.rsqrt(column[k:k + 1, :])
        pivot_row = value[k:k + 1, :] * scale
        weights = jnp.where(row > k, column, 0.0) * scale
        value = jnp.where(row == k, pivot_row, value - weights * pivot_row)
    corner = value[:, width:2 * width]
    upper[here, :] = dot(corner, block, PLAIN, HIGHEST)
    inverse[here, :] = dot(corner, target, PLAIN, HIGHEST)


def kernel(chips, acts, slots, gain, branch, hidden, seed, basis, moment, grad_out, moment_out,
           stored, part_s, sum_s, normed, term, grad, part_q, sum_q, part_g, sum_g, part_c, sum_c,
           inverse, upper, stat_tile, stat_slots, stat_mid, stat_recv, stat_sent,
           other, above, held, *rest):
    rest = list(rest)
    chain_sems = [rest.pop(0) for _ in range(6)]
    scratch = [[rest.pop(0) for _ in range(n)] for n in (5, 5, 4, 4)]
    p = Place()
    tokens = stored.shape[0]
    blocks = tokens // 128

    barrier = pltpu.get_barrier_semaphore()
    peers = [p.along(axis, steps) for axis in range(2) for steps in range(1, SIDE)]
    peers += list(chain_peers(p, chips))
    for peer in peers:
        pl.semaphore_signal(barrier, inc=1, device_id=peer, device_id_type=MESH)

    count = lax.broadcasted_iota(jnp.int32, (R, seed.shape[1]), 0).astype(F32) + 1.0
    product = seed[...].astype(F32) * count
    levels = product - jnp.floor(product * (1.0 / 65521.0)) * 65521.0
    levels = jnp.where(levels < 0.0, levels + 65521.0, levels)
    levels = jnp.where(levels >= 65521.0, levels - 65521.0, levels)
    omega = ((levels - 32760.0) * (1.7320508 / 32760.0)).astype(BF16)
    part_s[...] = dot(hidden[...], omega, LAST)

    gains = gain[...].astype(F32)
    per_slot = acts.shape[1] // 128
    ones = jnp.ones((8, gains.shape[1]), F32)
    rows_of = [[], []]
    for block in range(blocks):
        here = pl.ds((block % per_slot) * 128, 128)
        values = acts[slots[0, block // per_slot], here, :].astype(F32)
        stored[pl.ds(block * 128, 128), :] = values
        upstream = gains * branch[block // per_slot, here, :].astype(F32)
        rows_of[0].append(dot(ones, values * values, LAST, HIGHEST)[0:1, :])
        rows_of[1].append(dot(ones, values * upstream, LAST, HIGHEST)[0:1, :])
    stat_tile[...] = jnp.concatenate(rows_of[0] + rows_of[1], 0)
    pl.semaphore_wait(barrier, len(peers))

    stats = Stats(p, stat_tile, stat_slots, stat_mid, stat_recv, stat_sent)
    first = Reduce(p, part_s, sum_s, scratch[0])
    second = Reduce(p, part_q, sum_q, scratch[1])
    square = Small(p, part_g, sum_g, scratch[2])
    cross = Small(p, part_c, sum_c, scratch[3])
    chain = Chain(p, chips, term, grad, other, above, held, chain_sems)

    stats.start()
    first.scatter_start()
    stats.middle()
    first.scatter_mid()
    total = stats.end()
    inverses = 1.0 / jnp.sqrt(total[0:blocks] / D + 1e-05)
    pulls = inverses * inverses * inverses * (total[blocks:2 * blocks] / D)
    line = lax.broadcasted_iota(jnp.int32, (blocks, gains.shape[1]), 0)
    for block in range(blocks):
        here = pl.ds(block * 128, 128)
        pick = jnp.where(line == block, 1.0, 0.0).astype(F32)
        scale = dot(inverses, pick, FIRST, HIGHEST)
        pull = dot(pulls, pick, FIRST, HIGHEST)
        values = stored[here, :]
        inside = pl.ds((block % per_slot) * 128, 128)
        upstream = gains * branch[block // per_slot, inside, :].astype(F32)
        term[here, :] = scale * upstream - values * pull
        normed[here, :] = (values * scale * gains).astype(BF16)
    chain.start()
    first.scatter_end()
    chain.slot(0)
    first.near_end()
    chain.slot(1)
    first.gather_start()
    chain.slot(2)
    first.gather_mid()
    chain.slot(3)
    first.gather_end()

    wide = normed[...]
    rows = sum(dot(wide, piece, FIRST) for piece in split(sum_s[...], 3))
    part_g[...] = dot(rows, rows, FIRST, HIGHEST)
    square.start()
    pieces = split(rows, 3)
    part_q[...] = sum(dot(wide, piece) for piece in pieces)
    second.scatter_start()
    part_c[...] = sum(dot(basis[...], piece, FIRST) for piece in pieces)
    cross.start()
    chain.slot(4)
    square.middle()
    second.scatter_mid()
    cross.middle()
    square.spread()
    second.scatter_end()
    chain.slot(5)
    square.end()
    factor_panel(0, sum_g, inverse, upper)
    second.near_end()
    cross.spread()
    factor_panel(1, sum_g, inverse, upper)
    second.gather_start()
    factor_panel(2, sum_g, inverse, upper)
    chain.slot(6)
    factor_panel(3, sum_g, inverse, upper)
    second.gather_mid()
    for panel in range(4, R // PANEL):
        factor_panel(panel, sum_g, inverse, upper)
    chain.end()
    grad_out[...] = grad[...].astype(BF16)
    cross.end()
    second.gather_end()

    mixed = 0.9 * sum(dot(piece, moment[...], FIRST) for piece in split(sum_c[...], 2))
    mixed = mixed + 0.1 * sum(dot(piece, hidden[...], FIRST) for piece in split(sum_q[...], 2))
    high, low = split(inverse[...], 2)
    mixed_high, mixed_low = split(mixed, 2)
    moment_out[...] = (dot(high, mixed_high) + dot(high, mixed_low) + dot(low, mixed_high)).astype(BF16)
    for job in (stats, first, second, square, cross, chain):
        job.finish()


def local(acts, act_slot, norm_gain, branch_grad, hidden_grad, sketch_seed, basis_old, moment_old):
    batches, rows, features = acts.shape[1:]
    tokens = batches * rows
    units = hidden_grad.shape[-1]
    chips = lax.axis_size("pipe") // 2
    vmem = pl.BlockSpec(memory_space=pltpu.VMEM)
    smem = pl.BlockSpec(memory_space=pltpu.SMEM)
    dma = pltpu.SemaphoreType.DMA
    tile = (2 * (tokens // 128), 128)
    whole = pltpu.VMEM((tokens, R), F32)
    square = pltpu.VMEM((R, R), F32)
    wide = pltpu.VMEM((tokens, features), F32)
    half = pltpu.VMEM((tokens // 2, features), F32)
    grad, moment = pl.pallas_call(
        functools.partial(kernel, chips),
        out_shape=(jax.ShapeDtypeStruct((tokens, features), BF16),
                   jax.ShapeDtypeStruct((R, units), BF16)),
        in_specs=[vmem, smem, vmem, vmem, vmem, vmem, vmem, vmem],
        out_specs=(vmem, vmem),
        scratch_shapes=[
            wide, whole, whole, pltpu.VMEM((tokens, features), BF16), wide, wide, whole, whole,
            square, square, square, square, square, square,
            pltpu.VMEM(tile, F32), pltpu.VMEM((2, SIDE - 1) + tile, F32), pltpu.VMEM(tile, F32),
            dma((2,)), dma((2,)),
            half, half, wide,
        ] + [dma((CHAIN,))] * 6
        + Reduce.scratch(tokens) + Reduce.scratch(tokens) + Small.scratch(R) + Small.scratch(R),
        compiler_params=pltpu.CompilerParams(collective_id=1, has_side_effects=True,
                                             vmem_limit_bytes=60 * 1024 * 1024),
        name="section_backward",
    )(acts[0], act_slot, norm_gain, branch_grad[0], hidden_grad[0].reshape(tokens, units),
      sketch_seed, basis_old[0], moment_old[0])
    return (grad.reshape(branch_grad.shape), moment[None])


def solution(mesh):
    in_specs = (
        P("pipe", None, None, "dp"),
        P("pipe", None),
        P("pipe", "dp"),
        P("pipe", None, None, "dp"),
        P("pipe", None, None, "dp"),
        P("pipe", "dp"),
        P("pipe", "dp", None),
        P("pipe", None, "dp"),
    )
    out_specs = (P("pipe", None, None, "dp"), P("pipe", None, "dp"))
    return jax.shard_map(local, mesh=mesh, in_specs=in_specs, out_specs=out_specs, check_vma=False)
```

time: 745 us -> 114 us (0.15)
  waiting for transfers between devices: 458 us -> 0 us
  blocking collectives: 152 us -> 0 us
  Pallas kernels: 0 us -> 103 us
  other arithmetic: 74.3 us -> 0 us
  starting transfers between devices: 20.7 us -> 0 us
  between operations: 15.3 us -> 0.64 us
  matrix products: 13.8 us -> 0 us
    psum x3 -> x0, waiting for transfers between devices: 430 us -> none  [the longest x1 151 us: local(): lax.psum(jnp.dot(sketch_rows.T, sketch_rows, precision=highest), 'dp')]
    psum x1 -> x0, blocking collectives: 152 us -> none  [local(): lax.psum((jnp.sum(stored * stored, -1, keepdims=True), jnp.sum(stored * u...]
    pallas_call x0 -> x1, Pallas kernels: none -> 103 us  [local(): pl.pallas_call(functools.partial(kernel, chips), out_shape=(jax.ShapeDtyp...]
    another operation x9 -> x0, other arithmetic: 53.7 us -> none  [the longest x6 34 us: local(): factor = jnp.linalg.cholesky(gram_matrix)]
    ppermute x7 -> x0, waiting for transfers between devices: 28.1 us -> none  [passed_along(): lax.ppermute(value, axis, [(source, source + steps) for source in range(l...]
    ppermute x7 -> x0, starting transfers between devices: 20.6 us -> none  [passed_along(): lax.ppermute(value, axis, [(source, source + steps) for source in range(l...]
    add x7 -> x0, other arithmetic: 14.1 us -> none  [the longest x6 14.1 us: local(): current = term + passed_along(current, 'pipe', -1)]
    dot_general x7 -> x0, matrix products: 12.3 us -> none  [the longest x1 2.85 us: local(): lax.dot_general(projected, hidden.astype(jnp.float32), (((0,), (0,)), (()...]
  transfers between devices with their start and end apart: 10 -> 0, of which waited for: 6 -> 0; matrix products, arithmetic and copies ran while one was open for 11% -> 0% of each run, Pallas kernels for 0% -> 0%
where the time goes in v2:
time: 114 us; the launch traced here: 113 us
  Pallas kernels  103 us (90%)
  local copies, waits for them, and re-layouts  9.32 us (8%)
    pallas_call x1, Pallas kernels, local(): pl.pallas_call(functools.partial(kernel, chips), out_shape=(jax.ShapeDtyp...  103 us
    unnamed x4, local copies, waits for them, and re-layouts  9.32 us

profile of v2, /device:TPU:6, one launch (start us, length us, event | category | flops | bytes accessed | tf_op | source)
XLA Modules:
  0.0 113.4 jit_solution(14517060666629976831)
XLA Ops:
  0.6 2.0 %copy.11 = bf16[1,256,832]{2,1,0:T(8,128)(2,1)} copy(bf16[1,256,832]{1,2,0:T(8,128)(2,1)} %param.15) | data formatting | bytes 851968 | tf_op args[7]
  2.6 3.5 %copy.10 = bf16[1,4,256,832]{3,2,1,0:T(8,128)(2,1)} copy(bf16[1,4,256,832]{2,3,1,0:T(8,128)(2,1)} %param.12) | data formatting | bytes 3407872 | tf_op args[4]
  6.1 103.5 %section_backward.1 = (bf16[1024,256]{1,0:T(8,128)(2,1)}, bf16[256,832]{1,0:T(8,128)(2,1)}) custom-call(bf16[4,256,256]{2,1,0:T(8,128)(2,1)} %bitcast.9, s32[1,4]{1,0:T(1,128)} %slots.1, bf16[1,256]{1,0:T(2,128)(2,1)} %gain.1, bf16[4,256,256]{2,1,0:T(8,128)(2,1)} %bitcast.10, bf16[1024,832]{1,0:T(8,128)(2,1)} %bitcast.7, s32[1,832]{1,0:T(1,128)} %seed.1, ...), custom_call_target="tpu_custom_call" | custom-call | tf_op jit(solution)/shard_map/section_backward/pallas_call | solution.py:518
  109.6 2.0 %copy.12 = bf16[1,256,832]{1,2,0:T(8,128)(2,1)} copy(bf16[1,256,832]{2,1,0:T(8,128)(2,1)} %bitcast.12) | data formatting | bytes 851968
  111.5 1.9 %copy.14 = bf16[1,4,256,256]{3,2,1,0:T(8,128)(2,1)} copy(bf16[1,4,256,256]{3,2,1,0:T(8,128)(2,1)} %bitcast.11) | data formatting | bytes 1048576

commit v3 on v2

--- a/solution.py
+++ b/solution.py
@@ -15,7 +15,9 @@
 BF16 = jnp.bfloat16
 SIDE = 8
 CHAIN = 4
-PANEL = 32
+PANEL = 64
+GROUP = 8
+HALVES = 2
 FIRST = ((0,), (0,))
 LAST = ((1,), (1,))
 PLAIN = ((1,), (0,))
@@ -354,6 +356,36 @@
             (((p.x + chips - 1) % chips) * 2 + p.core, p.dp))
 
 
+def eliminate(value, width, row):
+    for k in range(0, width, GROUP):
+        columns = [jnp.broadcast_to(value[:, k + j:k + j + 1], value.shape) for j in range(GROUP)]
+        scales, low, uppers, weights = [], {}, [], []
+        for j in range(GROUP):
+            pivot = columns[j][k + j:k + j + 1, :]
+            for m in range(j):
+                pivot = pivot - low[j, m] * low[j, m]
+            scales.append(lax.rsqrt(pivot))
+            for i in range(j + 1, GROUP):
+                entry = columns[j][k + i:k + i + 1, :]
+                for m in range(j):
+                    entry = entry - low[i, m] * low[j, m]
+                low[i, j] = entry * scales[j]
+        for j in range(GROUP):
+            upper, weight = value[k + j:k + j + 1, :], columns[j]
+            for m in range(j):
+                upper = upper - low[j, m] * uppers[m]
+                weight = weight - weights[m] * low[j, m]
+            uppers.append(upper * scales[j])
+            weights.append(weight * scales[j])
+        updated = value
+        for j in range(GROUP):
+            updated = updated - weights[j] * uppers[j]
+        for j in range(GROUP):
+            updated = jnp.where(row == k + j, uppers[j], updated)
+        value = jnp.where(row < k, value, updated)
+    return value
+
+
 def factor_panel(panel, gram, inverse, upper):
     width = PANEL
     start = panel * width
@@ -374,12 +406,7 @@
     if shift:
         tile = pltpu.roll(tile, 128 - shift, 1)
     value = jnp.where(lane < width, tile, jnp.where(lane == row + width, 1.0, 0.0).astype(F32))
-    for k in range(width):
-        column = jnp.broadcast_to(value[:, k:k + 1], (width, 128))
-        scale = lax.rsqrt(column[k:k + 1, :])
-        pivot_row = value[k:k + 1, :] * scale
-        weights = jnp.where(row > k, column, 0.0) * scale
-        value = jnp.where(row == k, pivot_row, value - weights * pivot_row)
+    value = eliminate(value, width, row)
     corner = value[:, width:2 * width]
     upper[here, :] = dot(corner, block, PLAIN, HIGHEST)
     inverse[here, :] = dot(corner, target, PLAIN, HIGHEST)
@@ -391,7 +418,9 @@
            other, above, held, *rest):
     rest = list(rest)
     chain_sems = [rest.pop(0) for _ in range(6)]
-    scratch = [[rest.pop(0) for _ in range(n)] for n in (5, 5, 4, 4)]
+    firsts = [[rest.pop(0) for _ in range(5)] for _ in range(HALVES)]
+    seconds = [[rest.pop(0) for _ in range(5)] for _ in range(HALVES)]
+    scratch = [[rest.pop(0) for _ in range(4)] for _ in range(2)]
     p = Place()
     tokens = stored.shape[0]
     blocks = tokens // 128
@@ -408,7 +437,8 @@
     levels = jnp.where(levels < 0.0, levels + 65521.0, levels)
     levels = jnp.where(levels >= 65521.0, levels - 65521.0, levels)
     omega = ((levels - 32760.0) * (1.7320508 / 32760.0)).astype(BF16)
-    part_s[...] = dot(hidden[...], omega, LAST)
+    for batch in range(hidden.shape[0]):
+        part_s[pl.ds(batch * R, R), :] = dot(omega, hidden[batch])
 
     gains = gain[...].astype(F32)
     per_slot = acts.shape[1] // 128
@@ -425,16 +455,24 @@
     pl.semaphore_wait(barrier, len(peers))
 
     stats = Stats(p, stat_tile, stat_slots, stat_mid, stat_recv, stat_sent)
-    first = Reduce(p, part_s, sum_s, scratch[0])
-    second = Reduce(p, part_q, sum_q, scratch[1])
-    square = Small(p, part_g, sum_g, scratch[2])
-    cross = Small(p, part_c, sum_c, scratch[3])
+    share = tokens // HALVES
+    spans = [pl.ds(index * share, share) for index in range(HALVES)]
+    first = [Reduce(p, part_s.at[span], sum_s.at[span], own) for span, own in zip(spans, firsts)]
+    second = [Reduce(p, part_q.at[span], sum_q.at[span], own) for span, own in zip(spans, seconds)]
+    square = Small(p, part_g, sum_g, scratch[0])
+    cross = Small(p, part_c, sum_c, scratch[1])
     chain = Chain(p, chips, term, grad, other, above, held, chain_sems)
-
+    per_part = hidden.shape[0] // HALVES
+
+    def every(jobs, step):
+        for job in jobs:
+            getattr(job, step)()
+
+    every(first, "scatter_start")
     stats.start()
-    first.scatter_start()
+    every(first, "scatter_mid")
     stats.middle()
-    first.scatter_mid()
+    every(first, "scatter_end")
     total = stats.end()
     inverses = 1.0 / jnp.sqrt(total[0:blocks] / D + 1e-05)
     pulls = inverses * inverses * inverses * (total[blocks:2 * blocks] / D)
@@ -449,56 +487,62 @@
         upstream = gains * branch[block // per_slot, inside, :].astype(F32)
         term[here, :] = scale * upstream - values * pull
         normed[here, :] = (values * scale * gains).astype(BF16)
+    every(first, "near_end")
     chain.start()
-    first.scatter_end()
+    every(first, "gather_start")
     chain.slot(0)
-    first.near_end()
+    every(first, "gather_mid")
     chain.slot(1)
-    first.gather_start()
+
+    rows = jnp.zeros((R, gains.shape[1]), F32)
+    for index in range(HALVES):
+        first[index].gather_end()
+        for batch in range(index * per_part, (index + 1) * per_part):
+            wide = normed[pl.ds(batch * acts.shape[1], acts.shape[1]), :]
+            for piece in split(sum_s[pl.ds(batch * R, R), :], 3):
+                rows = rows + dot(piece, wide)
+    pieces = split(rows, 3)
+    for index in range(HALVES):
+        part_q[spans[index], :] = sum(dot(normed[spans[index], :], piece, LAST) for piece in pieces)
+        second[index].scatter_start()
+    part_g[...] = dot(rows, rows, LAST, HIGHEST)
+    square.start()
     chain.slot(2)
-    first.gather_mid()
+    part_c[...] = sum(dot(piece, basis[...]) for piece in pieces)
+    every(second, "scatter_mid")
+    square.middle()
+    cross.start()
     chain.slot(3)
-    first.gather_end()
-
-    wide = normed[...]
-    rows = sum(dot(wide, piece, FIRST) for piece in split(sum_s[...], 3))
-    part_g[...] = dot(rows, rows, FIRST, HIGHEST)
-    square.start()
-    pieces = split(rows, 3)
-    part_q[...] = sum(dot(wide, piece) for piece in pieces)
-    second.scatter_start()
-    part_c[...] = sum(dot(basis[...], piece, FIRST) for piece in pieces)
-    cross.start()
+    every(second, "scatter_end")
+    square.spread()
     chain.slot(4)
-    square.middle()
-    second.scatter_mid()
+    every(second, "near_end")
     cross.middle()
-    square.spread()
-    second.scatter_end()
-    chain.slot(5)
     square.end()
     factor_panel(0, sum_g, inverse, upper)
-    second.near_end()
+    every(second, "gather_start")
     cross.spread()
     factor_panel(1, sum_g, inverse, upper)
-    second.gather_start()
+    chain.slot(5)
     factor_panel(2, sum_g, inverse, upper)
+    every(second, "gather_mid")
+    factor_panel(3, sum_g, inverse, upper)
     chain.slot(6)
-    factor_panel(3, sum_g, inverse, upper)
-    second.gather_mid()
-    for panel in range(4, R // PANEL):
-        factor_panel(panel, sum_g, inverse, upper)
     chain.end()
-    grad_out[...] = grad[...].astype(BF16)
+    grad_out[...] = grad[...]
     cross.end()
-    second.gather_end()
-
-    mixed = 0.9 * sum(dot(piece, moment[...], FIRST) for piece in split(sum_c[...], 2))
-    mixed = mixed + 0.1 * sum(dot(piece, hidden[...], FIRST) for piece in split(sum_q[...], 2))
+
+    mixed = 0.9 * sum(dot(moment[...], piece, LAST) for piece in split(sum_c[...], 2))
     high, low = split(inverse[...], 2)
+    for index in range(HALVES):
+        second[index].gather_end()
+        for batch in range(index * per_part, (index + 1) * per_part):
+            for piece in split(sum_q[pl.ds(batch * acts.shape[1], acts.shape[1]), :], 2):
+                mixed = mixed + 0.1 * dot(hidden[batch], piece)
     mixed_high, mixed_low = split(mixed, 2)
-    moment_out[...] = (dot(high, mixed_high) + dot(high, mixed_low) + dot(low, mixed_high)).astype(BF16)
-    for job in (stats, first, second, square, cross, chain):
+    moment_out[...] = (dot(mixed_high, high, LAST) + dot(mixed_low, high, LAST)
+                       + dot(mixed_high, low, LAST))
+    for job in (stats, *first, *second, square, cross, chain):
         job.finish()
 
 
@@ -517,8 +561,8 @@
     half = pltpu.VMEM((tokens // 2, features), F32)
     grad, moment = pl.pallas_call(
         functools.partial(kernel, chips),
-        out_shape=(jax.ShapeDtypeStruct((tokens, features), BF16),
-                   jax.ShapeDtypeStruct((R, units), BF16)),
+        out_shape=(jax.ShapeDtypeStruct((tokens, features), F32),
+                   jax.ShapeDtypeStruct((units, R), F32)),
         in_specs=[vmem, smem, vmem, vmem, vmem, vmem, vmem, vmem],
         out_specs=(vmem, vmem),
         scratch_shapes=[
@@ -528,13 +572,13 @@
             dma((2,)), dma((2,)),
             half, half, wide,
         ] + [dma((CHAIN,))] * 6
-        + Reduce.scratch(tokens) + Reduce.scratch(tokens) + Small.scratch(R) + Small.scratch(R),
+        + Reduce.scratch(tokens // HALVES) * (2 * HALVES) + Small.scratch(R) * 2,
         compiler_params=pltpu.CompilerParams(collective_id=1, has_side_effects=True,
                                              vmem_limit_bytes=60 * 1024 * 1024),
         name="section_backward",
-    )(acts[0], act_slot, norm_gain, branch_grad[0], hidden_grad[0].reshape(tokens, units),
-      sketch_seed, basis_old[0], moment_old[0])
-    return (grad.reshape(branch_grad.shape), moment[None])
+    )(acts[0], act_slot, norm_gain, branch_grad[0], hidden_grad[0].swapaxes(1, 2),
+      sketch_seed, basis_old[0], moment_old[0].T)
+    return (grad.astype(BF16).reshape(branch_grad.shape), moment.astype(BF16).T[None])
 
 
 def solution(mesh):

time: 114 us -> 95.4 us (0.84)
  Pallas kernels: 103 us -> 90.5 us
  local copies, waits for them, and re-layouts: 9.32 us -> 0.01 us
  other arithmetic: 0 us -> 2.95 us
    pallas_call x1, Pallas kernels: 103 us -> 90.5 us  [local(): pl.pallas_call(functools.partial(kernel, chips), out_shape=(jax.ShapeDtyp...]
    unnamed x4 -> x2, local copies, waits for them, and re-layouts: 9.32 us -> 0.01 us
    convert_element_type x0 -> x1, other arithmetic: none -> 2.15 us  [local(): grad.astype(BF16).reshape(branch_grad.shape)]
where the time goes in v3:
time: 95.4 us; the launch traced here: 94.1 us
  Pallas kernels  90.5 us (95%)
  other arithmetic  2.95 us (3%)
    pallas_call x1, Pallas kernels, local(): pl.pallas_call(functools.partial(kernel, chips), out_shape=(jax.ShapeDtyp...  90.5 us
    convert_element_type x1, other arithmetic, local(): grad.astype(BF16).reshape(branch_grad.shape)  2.15 us

profile of v3, /device:TPU:6, one launch (start us, length us, event | category | flops | bytes accessed | tf_op | source)
XLA Modules:
  0.0 94.1 jit_solution(8775607688865699419)
XLA Ops:
  0.6 90.5 %section_backward.1 = (f32[1024,256]{1,0:T(8,128)}, f32[832,256]{1,0:T(8,128)}) custom-call(bf16[4,256,256]{2,1,0:T(8,128)(2,1)} %bitcast.16, s32[1,4]{1,0:T(1,128)} %slots.1, bf16[1,256]{1,0:T(2,128)(2,1)} %gain.1, bf16[4,256,256]{2,1,0:T(8,128)(2,1)} %bitcast.17, bf16[4,832,256]{2,1,0:T(8,128)(2,1)} %bitcast.14, s32[1,832]{1,0:T(1,128)} %seed.1, ...), custom_call_target="tpu_custom_call" | custom-call | tf_op jit(solution)/shard_map/section_backward/pallas_call | solution.py:562
  91.1 0.0 copy-start
  91.1 2.1 %convert_element_type.6 = bf16[1024,256]{1,0:T(8,128)(2,1)} convert(f32[1024,256]{1,0:T(8,128)} %get-tuple-element.4) | non-fusion elementwise | flops 262144 | bytes 1572864 | tf_op jit(solution)/shard_map/convert_element_type | solution.py:581
  93.3 0.0 copy-done
  93.3 0.8 convert_bitcast_fusion
Async XLA Ops:
  91.1 2.2 %copy-start = (f32[832,256]{1,0:T(8,128)S(1)}, f32[832,256]{1,0:T(8,128)}, u32[]{:S(2)}) copy-start(f32[832,256]{1,0:T(8,128)} %get-tuple-element.5) | copy-start | bytes 2555908

commit v4 on v3

--- a/solution.py
+++ b/solution.py
@@ -35,6 +35,11 @@
         parts.append(part)
         value = value - part.astype(F32)
     return parts
+
+
+def row_sums(values):
+    ones = jnp.ones((8, values.shape[1]), BF16)
+    return sum(dot(ones, piece, LAST) for piece in split(values, 3))[0:1, :]
 
 
 class Place:
@@ -386,13 +391,21 @@
     return value
 
 
+def gram_rows(panel, gram):
+    if panel < 2:
+        right = gram[128:192, 128 * panel:128 * panel + 128]
+        return jnp.concatenate([gram[PANEL * panel:PANEL * (panel + 1), 0:128], right], 1)
+    right = gram[PANEL * (panel - 2):PANEL * (panel - 1), 128:256]
+    return jnp.concatenate([jnp.zeros((PANEL, 128), F32), right], 1)
+
+
 def factor_panel(panel, gram, inverse, upper):
     width = PANEL
     start = panel * width
     here = pl.ds(start, width)
     row = lax.broadcasted_iota(jnp.int32, (width, 128), 0)
     lane = lax.broadcasted_iota(jnp.int32, (width, 128), 1)
-    block = gram[here, :]
+    block = gram_rows(panel, gram)
     wide = lax.broadcasted_iota(jnp.int32, (width, R), 1)
     deep = lax.broadcasted_iota(jnp.int32, (width, R), 0)
     target = jnp.where(wide == deep + start, 1.0, 0.0).astype(F32)
@@ -424,6 +437,7 @@
     p = Place()
     tokens = stored.shape[0]
     blocks = tokens // 128
+    per_part = hidden.shape[0] // HALVES
 
     barrier = pltpu.get_barrier_semaphore()
     peers = [p.along(axis, steps) for axis in range(2) for steps in range(1, SIDE)]
@@ -437,21 +451,12 @@
     levels = jnp.where(levels < 0.0, levels + 65521.0, levels)
     levels = jnp.where(levels >= 65521.0, levels - 65521.0, levels)
     omega = ((levels - 32760.0) * (1.7320508 / 32760.0)).astype(BF16)
-    for batch in range(hidden.shape[0]):
-        part_s[pl.ds(batch * R, R), :] = dot(omega, hidden[batch])
-
-    gains = gain[...].astype(F32)
-    per_slot = acts.shape[1] // 128
-    ones = jnp.ones((8, gains.shape[1]), F32)
-    rows_of = [[], []]
-    for block in range(blocks):
-        here = pl.ds((block % per_slot) * 128, 128)
-        values = acts[slots[0, block // per_slot], here, :].astype(F32)
-        stored[pl.ds(block * 128, 128), :] = values
-        upstream = gains * branch[block // per_slot, here, :].astype(F32)
-        rows_of[0].append(dot(ones, values * values, LAST, HIGHEST)[0:1, :])
-        rows_of[1].append(dot(ones, values * upstream, LAST, HIGHEST)[0:1, :])
-    stat_tile[...] = jnp.concatenate(rows_of[0] + rows_of[1], 0)
+
+    def sketch_share(index):
+        for batch in range(index * per_part, (index + 1) * per_part):
+            part_s[pl.ds(batch * R, R), :] = dot(omega, hidden[batch])
+
+    sketch_share(0)
     pl.semaphore_wait(barrier, len(peers))
 
     stats = Stats(p, stat_tile, stat_slots, stat_mid, stat_recv, stat_sent)
@@ -462,13 +467,26 @@
     square = Small(p, part_g, sum_g, scratch[0])
     cross = Small(p, part_c, sum_c, scratch[1])
     chain = Chain(p, chips, term, grad, other, above, held, chain_sems)
-    per_part = hidden.shape[0] // HALVES
 
     def every(jobs, step):
         for job in jobs:
             getattr(job, step)()
 
-    every(first, "scatter_start")
+    first[0].scatter_start()
+    for index in range(1, HALVES):
+        sketch_share(index)
+        first[index].scatter_start()
+    gains = gain[...].astype(F32)
+    per_slot = acts.shape[1] // 128
+    rows_of = [[], []]
+    for block in range(blocks):
+        here = pl.ds((block % per_slot) * 128, 128)
+        values = acts[slots[0, block // per_slot], here, :].astype(F32)
+        stored[pl.ds(block * 128, 128), :] = values
+        upstream = gains * branch[block // per_slot, here, :].astype(F32)
+        rows_of[0].append(row_sums(values * values))
+        rows_of[1].append(row_sums(values * upstream))
+    stat_tile[...] = jnp.concatenate(rows_of[0] + rows_of[1], 0)
     stats.start()
     every(first, "scatter_mid")
     stats.middle()
@@ -501,28 +519,32 @@
             wide = normed[pl.ds(batch * acts.shape[1], acts.shape[1]), :]
             for piece in split(sum_s[pl.ds(batch * R, R), :], 3):
                 rows = rows + dot(piece, wide)
-    pieces = split(rows, 3)
+    pieces = split(rows, 2)
     for index in range(HALVES):
         part_q[spans[index], :] = sum(dot(normed[spans[index], :], piece, LAST) for piece in pieces)
         second[index].scatter_start()
-    part_g[...] = dot(rows, rows, LAST, HIGHEST)
+    full = dot(rows, rows, LAST, HIGHEST)
+    part_g[0:128, 0:128] = full[0:128, 0:128]
+    part_g[0:128, 128:256] = full[128:256, 128:256]
+    part_g[128:192, 0:128] = full[0:64, 128:256]
+    part_g[128:192, 128:256] = full[64:128, 128:256]
     square.start()
     chain.slot(2)
     part_c[...] = sum(dot(piece, basis[...]) for piece in pieces)
     every(second, "scatter_mid")
     square.middle()
-    cross.start()
     chain.slot(3)
     every(second, "scatter_end")
     square.spread()
+    cross.start()
     chain.slot(4)
     every(second, "near_end")
-    cross.middle()
     square.end()
     factor_panel(0, sum_g, inverse, upper)
+    cross.middle()
     every(second, "gather_start")
+    factor_panel(1, sum_g, inverse, upper)
     cross.spread()
-    factor_panel(1, sum_g, inverse, upper)
     chain.slot(5)
     factor_panel(2, sum_g, inverse, upper)
     every(second, "gather_mid")
@@ -546,6 +568,24 @@
         job.finish()
 
 
+def round_kernel(grad, moment, grad_out, moment_out):
+    grad_out[...] = grad[...].astype(BF16)
+    moment_out[...] = moment[...].astype(BF16)
+
+
+def rounded(*arrays):
+    steps = 4
+    specs = [pl.BlockSpec((a.shape[0] // steps, a.shape[1]), lambda i: (i, 0)) for a in arrays]
+    return pl.pallas_call(
+        round_kernel,
+        grid=(steps,),
+        out_shape=tuple(jax.ShapeDtypeStruct(a.shape, BF16) for a in arrays),
+        in_specs=specs,
+        out_specs=tuple(specs),
+        name="round_outputs",
+    )(*arrays)
+
+
 def local(acts, act_slot, norm_gain, branch_grad, hidden_grad, sketch_seed, basis_old, moment_old):
     batches, rows, features = acts.shape[1:]
     tokens = batches * rows
@@ -557,6 +597,7 @@
     tile = (2 * (tokens // 128), 128)
     whole = pltpu.VMEM((tokens, R), F32)
     square = pltpu.VMEM((R, R), F32)
+    upper_blocks = pltpu.VMEM((R - PANEL, R), F32)
     wide = pltpu.VMEM((tokens, features), F32)
     half = pltpu.VMEM((tokens // 2, features), F32)
     grad, moment = pl.pallas_call(
@@ -567,18 +608,19 @@
         out_specs=(vmem, vmem),
         scratch_shapes=[
             wide, whole, whole, pltpu.VMEM((tokens, features), BF16), wide, wide, whole, whole,
-            square, square, square, square, square, square,
+            upper_blocks, upper_blocks, square, square, square, square,
             pltpu.VMEM(tile, F32), pltpu.VMEM((2, SIDE - 1) + tile, F32), pltpu.VMEM(tile, F32),
             dma((2,)), dma((2,)),
             half, half, wide,
         ] + [dma((CHAIN,))] * 6
-        + Reduce.scratch(tokens // HALVES) * (2 * HALVES) + Small.scratch(R) * 2,
+        + Reduce.scratch(tokens // HALVES) * (2 * HALVES) + Small.scratch(R - PANEL) + Small.scratch(R),
         compiler_params=pltpu.CompilerParams(collective_id=1, has_side_effects=True,
                                              vmem_limit_bytes=60 * 1024 * 1024),
         name="section_backward",
     )(acts[0], act_slot, norm_gain, branch_grad[0], hidden_grad[0].swapaxes(1, 2),
       sketch_seed, basis_old[0], moment_old[0].T)
-    return (grad.astype(BF16).reshape(branch_grad.shape), moment.astype(BF16).T[None])
+    grad, moment = rounded(grad, moment)
+    return (grad.reshape(branch_grad.shape), moment.T[None])
 
 
 def solution(mesh):

time: 95.4 us -> 93.4 us (0.979)
  other arithmetic: 2.95 us -> 0 us
  Pallas kernels: 90.5 us -> 91.9 us
    pallas_call x0 -> x1, Pallas kernels: none -> 3.49 us  [rounded(): pl.pallas_call(round_kernel, grid=(steps,), out_shape=tuple((jax.ShapeDty...]
    convert_element_type x1 -> x0, other arithmetic: 2.15 us -> none  [local(): grad.astype(BF16).reshape(branch_grad.shape)]
    pallas_call x1, Pallas kernels: 90.5 us -> 88.4 us  [local(): pl.pallas_call(functools.partial(kernel, chips), out_shape=(jax.ShapeDtyp...]
where the time goes in v4:
time: 93.4 us; the launch traced here: 92.5 us
  Pallas kernels  91.9 us (98%)
    pallas_call x1, Pallas kernels, local(): pl.pallas_call(functools.partial(kernel, chips), out_shape=(jax.ShapeDtyp...  88.4 us
    pallas_call x1, Pallas kernels, rounded(): pl.pallas_call(round_kernel, grid=(steps,), out_shape=tuple((jax.ShapeDty...  3.49 us

profile of v4, /device:TPU:6, one launch (start us, length us, event | category | flops | bytes accessed | tf_op | source)
XLA Modules:
  0.0 92.5 jit_solution(6402177267163069161)
XLA Ops:
  0.6 88.4 %section_backward.1 = (f32[1024,256]{1,0:T(8,128)}, f32[832,256]{1,0:T(8,128)}) custom-call(bf16[4,256,256]{2,1,0:T(8,128)(2,1)} %bitcast.14, s32[1,4]{1,0:T(1,128)} %slots.1, bf16[1,256]{1,0:T(2,128)(2,1)} %gain.1, bf16[4,256,256]{2,1,0:T(8,128)(2,1)} %bitcast.15, bf16[4,832,256]{2,1,0:T(8,128)(2,1)} %bitcast.13, s32[1,832]{1,0:T(1,128)} %seed.1, ...), custom_call_target="tpu_custom_call" | custom-call | tf_op jit(solution)/shard_map/section_backward/pallas_call | solution.py:603
  89.0 3.5 %round_outputs.1 = (bf16[1024,256]{1,0:T(8,128)(2,1)}, bf16[832,256]{1,0:T(8,128)(2,1)}) custom-call(f32[1024,256]{1,0:T(8,128)} %get-tuple-element.6.grad, f32[832,256]{1,0:T(8,128)} %get-tuple-element.7.moment), custom_call_target="tpu_custom_call" | custom-call | tf_op jit(solution)/shard_map/round_outputs/pallas_call | solution.py:579

commit v5 on v4

--- a/solution.py
+++ b/solution.py
@@ -542,13 +542,13 @@
     square.end()
     factor_panel(0, sum_g, inverse, upper)
     cross.middle()
+    factor_panel(1, sum_g, inverse, upper)
     every(second, "gather_start")
-    factor_panel(1, sum_g, inverse, upper)
+    factor_panel(2, sum_g, inverse, upper)
     cross.spread()
     chain.slot(5)
-    factor_panel(2, sum_g, inverse, upper)
+    factor_panel(3, sum_g, inverse, upper)
     every(second, "gather_mid")
-    factor_panel(3, sum_g, inverse, upper)
     chain.slot(6)
     chain.end()
     grad_out[...] = grad[...]

time: 93.4 us -> 93.8 us (level)
  no operation moved by 1% of the time
where the time goes in v5:
time: 93.8 us; the launch traced here: 92.6 us
  Pallas kernels  91.9 us (98%)
    pallas_call x1, Pallas kernels, local(): pl.pallas_call(functools.partial(kernel, chips), out_shape=(jax.ShapeDtyp...  88.4 us
    pallas_call x1, Pallas kernels, rounded(): pl.pallas_call(round_kernel, grid=(steps,), out_shape=tuple((jax.ShapeDty...  3.49 us

profile of v5, /device:TPU:6, one launch (start us, length us, event | category | flops | bytes accessed | tf_op | source)
XLA Modules:
  0.0 92.6 jit_solution(8289862075793604317)
XLA Ops:
  0.6 88.4 %section_backward.1 = (f32[1024,256]{1,0:T(8,128)}, f32[832,256]{1,0:T(8,128)}) custom-call(bf16[4,256,256]{2,1,0:T(8,128)(2,1)} %bitcast.14, s32[1,4]{1,0:T(1,128)} %slots.1, bf16[1,256]{1,0:T(2,128)(2,1)} %gain.1, bf16[4,256,256]{2,1,0:T(8,128)(2,1)} %bitcast.15, bf16[4,832,256]{2,1,0:T(8,128)(2,1)} %bitcast.13, s32[1,832]{1,0:T(1,128)} %seed.1, ...), custom_call_target="tpu_custom_call" | custom-call | tf_op jit(solution)/shard_map/section_backward/pallas_call | solution.py:603
  89.1 3.5 %round_outputs.1 = (bf16[1024,256]{1,0:T(8,128)(2,1)}, bf16[832,256]{1,0:T(8,128)(2,1)}) custom-call(f32[1024,256]{1,0:T(8,128)} %get-tuple-element.6.grad, f32[832,256]{1,0:T(8,128)} %get-tuple-element.7.moment), custom_call_target="tpu_custom_call" | custom-call | tf_op jit(solution)/shard_map/round_outputs/pallas_call | solution.py:579
